TPU v7x, 256 devices: a whole 4x4x8 slice. The times are simulated.
256 devices in a mesh: slab: 16 (over x, y), pencil: 16 (over z, core).
Axes of the slice: x: 4, y: 4, z: 8, core: 2. Of those that a mesh axis runs over, the one named last changes fastest.
Arguments:
- charges: bfloat16 [64, 131072], P(None, ('slab', 'pencil')), may hold values from -6 to 6
- cotangent: bfloat16 [64, 131072], P(None, ('slab', 'pencil')), may hold values from -6 to 6
- base_cell: int32 [3, 131072], P(None, ('slab', 'pencil')), may hold values from 0 to 63, as said below
- frac: float32 [3, 131072], P(None, ('slab', 'pencil')), may hold values from 0 to 1
- counts: int32 [256], P(('slab', 'pencil')), may hold values from 256 to 512, as said below
- filter_weights: float32 [32, 64], replicated, may hold values from -6 to 6
Outputs:
- potential: bfloat16 [64, 131072], P(None, ('slab', 'pencil'))
- charge_grad: bfloat16 [64, 131072], P(None, ('slab', 'pencil'))
- filter_grad: float32 [32, 64], replicated
Inputs may be any that keep to these rules, and one draw needn't show every extreme that they name: `base_cell`: slots d * 512 to (d + 1) * 512 - 1 belong to device d = slab index * (pencil axis size) + pencil index; their first cell index lies in the slab index's run of 4 cells and their second in the pencil index's run of 4 cells; the third is any cell. A device's live atoms are its first counts slots; some device's count is 512.
All inputs are finite; a program needn't handle non-finite values.
Results may differ from a plain program's by a relative error of at most 0.013.
Values may be sent and summed in bfloat16 or wider, within the bound.
A program may use at most 128 MiB of HBM per device.

v0:
```python
import jax
import jax.numpy as jnp
from jax import lax
from jax.sharding import PartitionSpec as P

N = 64
C = 64
NB = 32


ENV_SCALE = 40.0
ENV_WIDTH = 16.0


def passed_along(value, axis, steps):
    count = lax.axis_size(axis)
    pairs = [(source, (source + steps) % count) for source in range(count)]
    return lax.ppermute(value, axis, pairs)


def spline_weights(frac):
    remain = 1.0 - frac
    square = frac * frac
    cubed = square * frac
    weight_zero = remain * remain * remain / 6.0
    weight_one = (3.0 * cubed - 6.0 * square + 4.0) / 6.0
    weight_two = (-3.0 * cubed + 3.0 * square + 3.0 * frac + 1.0) / 6.0
    weight_three = cubed / 6.0
    return jnp.stack([weight_zero, weight_one, weight_two, weight_three], axis=1)


def stencil_local(base_cell, frac, live, x_first, y_first, span_y):
    weights = spline_weights(frac)
    offsets = jnp.arange(64, dtype=jnp.int32)
    along_x = jnp.repeat(weights[0], 16, axis=0)
    along_y = jnp.tile(jnp.repeat(weights[1], 4, axis=0), (4, 1))
    along_z = jnp.tile(weights[2], (16, 1))
    stencil = along_x * along_y * along_z * live[None, :]
    local_x = base_cell[0][None, :] - x_first + offsets[:, None] // 16
    local_y = base_cell[1][None, :] - y_first + offsets[:, None] // 4 % 4
    local_z = (base_cell[2][None, :] + offsets[:, None] % 4) % N
    cell_ids = (local_x * (span_y + 3) + local_y) * N + local_z
    return (cell_ids, stencil)


def frequencies(positions):
    return jnp.where(positions < N // 2, positions, positions - N).astype(jnp.float32)


def filter_shells(y_first, z_first, y_count, z_count):
    freq_x = frequencies(jnp.arange(N, dtype=jnp.int32))
    freq_y = frequencies(y_first + jnp.arange(y_count, dtype=jnp.int32))
    freq_z = frequencies(z_first + jnp.arange(z_count, dtype=jnp.int32))
    kappa_sq = (
        freq_x[:, None, None] * freq_x[:, None, None]
        + freq_y[None, :, None] * freq_y[None, :, None]
        + freq_z[None, None, :] * freq_z[None, None, :]
    )
    kappa = jnp.sqrt(kappa_sq)
    envelope = ENV_SCALE * ENV_WIDTH / (ENV_WIDTH + kappa_sq)
    spacing = N / (2.0 * NB)
    centers = (jnp.arange(NB, dtype=jnp.float32) + 0.5) * spacing
    shells = envelope[..., None] * jnp.exp(-jnp.square((kappa[..., None] - centers) / spacing))
    return shells.reshape(N * y_count * z_count, NB)


def dft_tables(length):
    indices = jnp.arange(length, dtype=jnp.int32)
    phases = indices[:, None] * indices[None, :] % length
    angles = phases.astype(jnp.float32) * (2.0 * jnp.pi / length)
    return (jnp.cos(angles), jnp.sin(angles))


def contract(operand, matrix, pattern):
    if operand.dtype == jnp.bfloat16:
        table_high = matrix.astype(jnp.bfloat16)
        table_low = (matrix - table_high.astype(jnp.float32)).astype(jnp.bfloat16)
        first = jnp.einsum(pattern, operand, table_high, preferred_element_type=jnp.float32)
        second = jnp.einsum(pattern, operand, table_low, preferred_element_type=jnp.float32)
        return first + second
    return jnp.einsum(pattern, operand, matrix, precision=lax.Precision.HIGHEST)


def transform(values, pattern, inverse, real_in, real_out):
    cosines, sines = dft_tables(N)
    direction = 1.0 if inverse else -1.0
    factor = 1.0 / N if inverse else 1.0
    if real_in:
        real_part = values
        new_real = contract(real_part, cosines, pattern)
        new_imag = direction * contract(real_part, sines, pattern)
    else:
        halfway = values.shape[-1] // 2
        real_part = values[..., :halfway]
        imag_part = values[..., halfway:]
        new_real = contract(real_part, cosines, pattern) - direction * contract(
            imag_part, sines, pattern
        )
        if real_out:
            return new_real * factor
        new_imag = contract(imag_part, cosines, pattern) + direction * contract(
            real_part, sines, pattern
        )
    return jnp.concatenate([new_real, new_imag], axis=-1) * factor


def spread(values, cell_ids, stencil, span_x, span_y, blocks_run):
    channels = values.shape[1]
    total_cells = (span_x + 3) * (span_y + 3) * N

    def add_block(number, totals):
        block_vals = values.astype(jnp.float32)
        products = stencil[:, :, None] * block_vals[None, :, :]
        return totals.at[cell_ids.reshape(-1)].add(products.reshape(-1, channels))

    totals = lax.fori_loop(
        0, blocks_run, add_block, jnp.zeros((total_cells, channels), jnp.float32)
    )
    totals = totals.reshape(span_x + 3, span_y + 3, N, channels)
    rim_planes = passed_along(totals[span_x:].astype(jnp.bfloat16), "slab", 1).astype(jnp.float32)
    totals = totals[:span_x].at[:3].add(rim_planes)
    rim_rows = passed_along(totals[:, span_y:].astype(jnp.bfloat16), "pencil", 1).astype(
        jnp.float32
    )
    return totals[:, :span_y].at[:, :3].add(rim_rows)


def interpolate(grid_vals, cell_ids, stencil, blocks_run, block_len, slots):
    ghost_planes = passed_along(grid_vals[:3], "slab", -1)
    grid_vals = jnp.concatenate([grid_vals, ghost_planes], axis=0)
    ghost_rows = passed_along(grid_vals[:, :3], "pencil", -1)
    grid_vals = jnp.concatenate([grid_vals, ghost_rows], axis=1)
    channels = grid_vals.shape[3]
    flattened = grid_vals.reshape(-1, channels)

    def take_block(number, result):
        picked = (
            flattened[cell_ids.reshape(-1)].reshape(64, block_len, channels).astype(jnp.float32)
        )
        summed = jnp.sum(stencil[:, :, None] * picked, axis=0).astype(jnp.bfloat16)
        return summed

    return lax.fori_loop(0, blocks_run, take_block, jnp.zeros((slots, channels), jnp.bfloat16))


def forward_spectrum(density):
    section_one = transform(density, "xyzc,zk->xykc", False, True, False).astype(jnp.bfloat16)

    def along_y(block_vals):
        return transform(block_vals, "xyzc,yk->xkzc", False, False, False).astype(jnp.bfloat16)

    middle = along_y(lax.all_to_all(section_one, "pencil", split_axis=2, concat_axis=1, tiled=True))

    def along_x(block_vals):
        return transform(block_vals, "xyzc,xk->kyzc", False, False, False)

    return along_x(lax.all_to_all(middle, "slab", split_axis=1, concat_axis=0, tiled=True))


def back_to_cells(spectrum):
    section_one = transform(spectrum, "xyzc,xk->kyzc", True, False, False).astype(jnp.bfloat16)

    def along_y(block_vals):
        return transform(block_vals, "xyzc,yk->xkzc", True, False, False).astype(jnp.bfloat16)

    middle = along_y(lax.all_to_all(section_one, "slab", split_axis=0, concat_axis=1, tiled=True))

    def along_z(block_vals):
        return transform(block_vals, "xyzc,zk->xykc", True, False, True).astype(jnp.bfloat16)

    return along_z(lax.all_to_all(middle, "pencil", split_axis=1, concat_axis=2, tiled=True))


def per_device(charges, cotangent, base_cell, frac, counts, filter_weights):
    charges = charges.T
    cotangent = cotangent.T
    slab_index = lax.axis_index("slab")
    pencil_index = lax.axis_index("pencil")
    span_x = N // lax.axis_size("slab")
    span_y = N // lax.axis_size("pencil")
    slots = charges.shape[0]
    block_len = min(512, slots)
    live_count = counts[0]
    live = (jnp.arange(slots, dtype=jnp.int32) < live_count).astype(jnp.float32)
    cell_ids, stencil = stencil_local(
        base_cell, frac, live, slab_index * span_x, pencil_index * span_y, span_y
    )
    blocks_run = slots // block_len
    shells = filter_shells(slab_index * span_x, pencil_index * span_y, span_x, span_y)
    profile = jnp.dot(shells, filter_weights, precision=lax.Precision.HIGHEST).reshape(
        N, span_x, span_y, C
    )
    doubled = jnp.tile(profile, (1, 1, 1, 2))
    spectrum_q = forward_spectrum(spread(charges, cell_ids, stencil, span_x, span_y, blocks_run))
    potential = interpolate(
        back_to_cells(spectrum_q * doubled), cell_ids, stencil, blocks_run, block_len, slots
    )
    spectrum_g = forward_spectrum(spread(cotangent, cell_ids, stencil, span_x, span_y, blocks_run))
    correlation = (
        spectrum_g[..., :C] * spectrum_q[..., :C] + spectrum_g[..., C:] * spectrum_q[..., C:]
    )
    charge_grad = interpolate(
        back_to_cells(spectrum_g * doubled), cell_ids, stencil, blocks_run, block_len, slots
    )
    partial_grad = jnp.dot(
        shells.T, correlation.reshape(-1, C), precision=lax.Precision.HIGHEST
    ) / (N * N * N)
    filter_grad = lax.psum(partial_grad, ("slab", "pencil"))
    return (potential.T, charge_grad.T, filter_grad)


def solution(mesh):
    in_specs = (
        P(None, ("slab", "pencil")),
        P(None, ("slab", "pencil")),
        P(None, ("slab", "pencil")),
        P(None, ("slab", "pencil")),
        P(("slab", "pencil")),
        P(),
    )
    out_specs = (P(None, ("slab", "pencil")), P(None, ("slab", "pencil")), P())
    return jax.shard_map(
        per_device, mesh=mesh, in_specs=in_specs, out_specs=out_specs, check_vma=False
    )
```

profile of v0, /device:TPU:1, one launch (start us, length us, event | category | flops | bytes accessed | tf_op | source)
XLA Modules:
  0.0 876.0 jit_solution(3839491875228261354)
XLA Ops:
  6.2 12.0 %bitcast_multiply_fusion.1 = (f32[32768,64]{1,0:T(8,128)}, f32[32768,64]{1,0:T(8,128)}) fusion(f32[512,64]{1,0:T(8,128)S(1)} %copy.19, f32[32768]{0:T(1024)S(1)} %multiply_multiply_fusion, f32[512,64]{1,0:T(8,128)S(1)} %copy.28), kind=kLoop, calls=%fused_computation.9 | loop fusion | flops 4194304 | bytes 17170432 | tf_op jit(solution)/shard_map/while/body/eval_jaxpr/mul | solution.py:113
  18.2 174.7 %scatter_custom_fusion.1 = f32[3136,64]{1,0:T(8,128)S(1)} fusion(s32[32768]{0:T(1024)S(1)} %bitcast.346, f32[32768,64]{1,0:T(8,128)} %get-tuple-element.117, f32[]{:T(128)} %constant.266.clone.1), kind=kCustom, calls=%fused_computation.96 | custom fusion | flops 2097152 | bytes 803328 | tf_op jit(solution)/shard_map/while/body/eval_jaxpr/scatter-add | solution.py:114
  193.6 2.1 collective-permute-start.4
  195.8 174.7 %scatter_custom_fusion = f32[3136,64]{1,0:T(8,128)S(1)} fusion(s32[32768]{0:T(1024)S(1)} %bitcast.347, f32[32768,64]{1,0:T(8,128)} %get-tuple-element.116, f32[]{:T(128)} %constant.266.clone.1), kind=kCustom, calls=%fused_computation.98 | custom fusion | flops 2097152 | bytes 803328 | tf_op jit(solution)/shard_map/while/body/eval_jaxpr/scatter-add | solution.py:114
  371.2 1.8 collective-permute-start
  377.1 1.1 fusion.74
  380.6 2.1 add_dynamic-update-slice_fusion
  383.7 2.8 collective-permute-start.5
  386.5 1.3 add_dynamic-update-slice_fusion.1
  387.7 1.1 slice.316
  393.4 9.9 %all-to-all-start.4 = ((bf16[4,4,64,128]{3,1,0,2:T(4,128)(2,1)}), bf16[4,4,64,128]{3,1,0,2:T(4,128)(2,1)S(1)}, u32[]{:S(2)}, u32[]{:S(2)}) async-start(bf16[4,4,64,128]{3,1,0,2:T(4,128)(2,1)} %copy.29), calls=%async_computation.4 | async-start | bytes 524288 | tf_op jit(solution)/shard_map/all_to_all | solution.py:152
  406.8 8.1 all-to-all-done.4
  414.9 3.4 all-to-all-start
  418.4 1.2 fusion.115
  419.9 1.1 fusion.118
  421.5 8.0 all-to-all-done
  429.6 1.2 fusion.151
  431.1 1.1 fusion.154
  432.6 1.4 fusion.17
  434.0 1.4 fusion.19
  437.2 6.0 all-to-all-start.5
  443.3 1.4 fusion.3
  444.7 1.4 fusion.5
  447.9 3.2 all-to-all-done.5
  451.1 3.9 all-to-all-start.1
  455.8 1.1 fusion.106
  457.3 5.1 all-to-all-done.1
  464.4 1.4 fusion.23
  469.8 1.5 fusion.64
  474.7 4.4 all-to-all-start.2
  479.1 1.8 convolution_subtract_fusion
  482.7 3.8 all-to-all-done.2
  486.5 3.6 all-to-all-start.6
  491.2 1.2 fusion.127
  492.3 1.1 fusion.133
  493.5 1.1 fusion.130
  494.6 1.2 fusion.124
  495.8 1.6 all-to-all-done.6
  497.5 1.2 fusion.91
  499.0 1.2 fusion.94
  500.2 1.4 convolution_add_fusion.18
  501.6 1.4 convolution_add_fusion.16
  503.0 1.4 fusion.11
  504.4 1.4 fusion.13
  506.9 8.0 all-to-all-start.3
  515.0 1.4 convolution_add_fusion.4
  516.4 1.4 convolution_add_fusion.2
  520.0 6.7 all-to-all-done.3
  526.7 3.4 all-to-all-start.7
  530.2 1.6 fusion.161
  531.9 1.2 fusion.82
  533.4 7.7 all-to-all-done.7
  541.9 1.4 convolution_add_fusion.14
  543.7 2.3 collective-permute-start.2
  547.7 2.7 collective-permute-done.2
  550.4 1.2 collective-permute-start.3
  551.6 2.9 collective-permute-done.6
  556.8 1.3 fusion.48
  558.1 76.5 %psum.7 = f32[32,64]{1,0:T(8,128)} all-reduce(f32[32,64]{1,0:T(8,128)S(1)} %fusion.48), channel_id=1, replica_groups=mesh['slab'=16,'pencil'=16] {'slab','pencil'}, use_global_device_ids=true, to_apply=%region_4.5 | all-reduce | flops 2048 | bytes 16384 | tf_op jit(solution)/shard_map/psum | solution.py:208
  634.6 1.2 pad_maximum_fusion
  635.7 114.9 %gather_fusion = bf16[32768,64]{1,0:T(8,128)(2,1)} fusion(bf16[3136,64]{1,0:T(8,128)(2,1)S(1)} %bitcast.273, s32[32768]{0:T(1024)S(1)} %broadcast_clamp_fusion), kind=kCustom, calls=%fused_computation | custom fusion | bytes 8519680 | tf_op jit(solution)/shard_map/while/body/eval_jaxpr/gather | solution.py:138
  750.6 1.2 pad_maximum_fusion.1
  751.8 114.9 %gather_fusion.1 = bf16[32768,64]{1,0:T(8,128)(2,1)} fusion(bf16[3136,64]{1,0:T(8,128)(2,1)S(1)} %bitcast.272, s32[32768]{0:T(1024)S(1)} %broadcast_clamp_fusion), kind=kCustom, calls=%fused_computation.1 | custom fusion | bytes 8519680 | tf_op jit(solution)/shard_map/while/body/eval_jaxpr/gather | solution.py:138
  866.8 7.5 fusion
  (157 shorter events, 50.8 us)
Async XLA Ops:
  0.6 376.4 %copy-start = (f32[32,64]{1,0:T(8,128)S(1)}, f32[32,64]{1,0:T(8,128)}, u32[]{:S(2)}) copy-start(f32[32,64]{1,0:T(8,128)} %param.19) | copy-start | bytes 24580
  1.4 0.9 copy-start.10
  2.3 15.9 %copy-start.11 = (f32[512]{0:T(512)}, f32[512]{0:T(512)S(1)}, u32[]{:S(2)}) copy-start(f32[512]{0:T(512)S(1)} %fusion.301) | copy-start | bytes 6148
  6.1 189.7 %copy-start.5 = (s32[32768,1]{0,1:T(1,128)}, s32[32768,1]{0,1:T(1,128)S(1)}, u32[]{:S(2)}) copy-start(s32[32768,1]{0,1:T(1,128)S(1)} %compare_select_fusion) | copy-start | bytes 393220
  193.6 186.9 %collective-permute-start.4 = (bf16[3,7,64,64]{3,2,1,0:T(8,128)(2,1)}, bf16[3,7,64,64]{3,2,1,0:T(8,128)(2,1)}, u32[]{:S(2)}, u32[]{:S(2)}) collective-permute-start(bf16[3,7,64,64]{3,2,1,0:T(8,128)(2,1)} %bitcast.66), channel_id=1, source_target_pairs={{0,16},{16,32},{32,48},{48,64},{64,80},{80,96},{96,112},{112,128},... | collective-permute-start | bytes 516104 | tf_op jit(solution)/shard_map/ppermute | solution.py:18
  371.2 15.2 %collective-permute-start = (bf16[3,7,64,64]{3,2,1,0:T(8,128)(2,1)}, bf16[3,7,64,64]{3,2,1,0:T(8,128)(2,1)}, u32[]{:S(2)}, u32[]{:S(2)}) collective-permute-start(bf16[3,7,64,64]{3,2,1,0:T(8,128)(2,1)} %bitcast.21), channel_id=1, source_target_pairs={{0,16},{16,32},{32,48},{48,64},{64,80},{80,96},{96,112},{112,128},... | collective-permute-start | bytes 516104 | tf_op jit(solution)/shard_map/ppermute | solution.py:18
  375.9 29.1 %copy-start.13 = (f32[32]{0:T(128)}, f32[32]{0:T(128)S(1)}, u32[]{:S(2)}) copy-start(f32[32]{0:T(128)S(1)} %iota_add_fusion) | copy-start | bytes 388
  377.0 28.7 %copy-start.6 = (f32[64,4,4]{0,2,1:T(4,128)}, f32[64,4,4]{0,2,1:T(4,128)S(1)}, u32[]{:S(2)}) copy-start(f32[64,4,4]{0,2,1:T(4,128)S(1)} %get-tuple-element.128) | copy-start | bytes 12292
  377.0 28.7 %copy-start.8 = (f32[64,4,4]{0,2,1:T(4,128)}, f32[64,4,4]{0,2,1:T(4,128)S(1)}, u32[]{:S(2)}) copy-start(f32[64,4,4]{0,2,1:T(4,128)S(1)} %get-tuple-element.129) | copy-start | bytes 12292
  383.7 6.1 collective-permute-start.5
  388.9 14.4 %collective-permute-start.1 = (bf16[4,3,64,64]{3,2,1,0:T(8,128)(2,1)S(1)}, bf16[4,3,64,64]{3,2,1,0:T(8,128)(2,1)}, u32[]{:S(2)}, u32[]{:S(2)}) collective-permute-start(bf16[4,3,64,64]{3,2,1,0:T(8,128)(2,1)S(1)} %slice.473), channel_id=1, source_target_pairs={{0,1},{1,2},{2,3},{3,4},{4,5},{5,6},{6,7},{7,8},{8,9},{9,10},{10,1... | collective-permute-start | bytes 294920 | tf_op jit(solution)/shard_map/ppermute | solution.py:18
  393.4 21.5 %all-to-all-start.4 = ((bf16[4,4,64,128]{3,1,0,2:T(4,128)(2,1)}), bf16[4,4,64,128]{3,1,0,2:T(4,128)(2,1)S(1)}, u32[]{:S(2)}, u32[]{:S(2)}) async-start(bf16[4,4,64,128]{3,1,0,2:T(4,128)(2,1)} %copy.29), calls=%async_computation.4 | async-start | bytes 524288 | tf_op jit(solution)/shard_map/all_to_all | solution.py:152
  414.9 14.6 %all-to-all-start = ((bf16[4,4,64,128]{3,1,0,2:T(4,128)(2,1)}), bf16[4,4,64,128]{3,1,0,2:T(4,128)(2,1)S(1)}, u32[]{:S(2)}, u32[]{:S(2)}) async-start(bf16[4,4,64,128]{3,1,0,2:T(4,128)(2,1)} %copy.20), calls=%async_computation | async-start | bytes 524288 | tf_op jit(solution)/shard_map/all_to_all | solution.py:152
  437.2 13.9 %all-to-all-start.5 = ((bf16[4,64,4,128]{3,2,0,1:T(4,128)(2,1)}), bf16[4,64,4,128]{3,2,0,1:T(4,128)(2,1)S(1)}, u32[]{:S(2)}, u32[]{:S(2)}) async-start(bf16[4,64,4,128]{3,2,0,1:T(4,128)(2,1)} %copy.31), calls=%async_computation.5 | async-start | bytes 524288 | tf_op jit(solution)/shard_map/all_to_all | solution.py:157
  451.1 11.3 %all-to-all-start.1 = ((bf16[4,64,4,128]{3,2,0,1:T(4,128)(2,1)}), bf16[4,64,4,128]{3,2,0,1:T(4,128)(2,1)S(1)}, u32[]{:S(2)}, u32[]{:S(2)}) async-start(bf16[4,64,4,128]{3,2,0,1:T(4,128)(2,1)} %copy.22), calls=%async_computation.1 | async-start | bytes 524288 | tf_op jit(solution)/shard_map/all_to_all | solution.py:157
  474.7 11.9 %all-to-all-start.2 = ((bf16[64,4,4,128]{3,2,1,0:T(4,128)(2,1)}), bf16[64,4,4,128]{3,2,1,0:T(4,128)(2,1)}, u32[]{:S(2)}, u32[]{:S(2)}) async-start(bf16[64,4,4,128]{3,2,1,0:T(4,128)(2,1)} %copy.24), calls=%async_computation.2 | async-start | bytes 524288 | tf_op jit(solution)/shard_map/all_to_all | solution.py:166
  486.5 10.9 %all-to-all-start.6 = ((bf16[64,4,4,128]{3,2,1,0:T(4,128)(2,1)}), bf16[64,4,4,128]{3,2,1,0:T(4,128)(2,1)S(1)}, u32[]{:S(2)}, u32[]{:S(2)}) async-start(bf16[64,4,4,128]{3,2,1,0:T(4,128)(2,1)} %copy.33), calls=%async_computation.6 | async-start | bytes 524288 | tf_op jit(solution)/shard_map/all_to_all | solution.py:166
  501.6 28.6 %copy-start.12 = (f32[512]{0:T(512)S(1)}, f32[512]{0:T(512)}, u32[]{:S(2)}) copy-start(f32[512]{0:T(512)} %copy-done.11) | copy-start | bytes 6148
  506.9 19.8 %all-to-all-start.3 = ((bf16[4,64,4,128]{3,2,0,1:T(4,128)(2,1)}), bf16[4,64,4,128]{3,2,0,1:T(4,128)(2,1)S(1)}, u32[]{:S(2)}, u32[]{:S(2)}) async-start(bf16[4,64,4,128]{3,2,0,1:T(4,128)(2,1)} %copy.26), calls=%async_computation.3 | async-start | bytes 524288 | tf_op jit(solution)/shard_map/all_to_all | solution.py:171
  518.5 38.3 %copy-start.7 = (f32[64,4,4]{0,2,1:T(4,128)S(1)}, f32[64,4,4]{0,2,1:T(4,128)}, u32[]{:S(2)}) copy-start(f32[64,4,4]{0,2,1:T(4,128)} %copy-done.6) | copy-start | bytes 12292
  518.5 38.3 %copy-start.9 = (f32[64,4,4]{0,2,1:T(4,128)S(1)}, f32[64,4,4]{0,2,1:T(4,128)}, u32[]{:S(2)}) copy-start(f32[64,4,4]{0,2,1:T(4,128)} %copy-done.8) | copy-start | bytes 12292
  526.7 14.4 %all-to-all-start.7 = ((bf16[4,64,4,128]{3,2,0,1:T(4,128)(2,1)}), bf16[4,64,4,128]{3,2,0,1:T(4,128)(2,1)S(1)}, u32[]{:S(2)}, u32[]{:S(2)}) async-start(bf16[4,64,4,128]{3,2,0,1:T(4,128)(2,1)} %copy.35), calls=%async_computation.7 | async-start | bytes 524288 | tf_op jit(solution)/shard_map/all_to_all | solution.py:171
  543.7 6.6 collective-permute-start.2
  546.8 7.8 collective-permute-start.6
  550.4 84.2 %collective-permute-start.3 = (bf16[7,3,64,64]{3,2,1,0:T(8,128)(2,1)S(1)}, bf16[7,3,64,64]{3,2,1,0:T(8,128)(2,1)}, u32[]{:S(2)}, u32[]{:S(2)}) collective-permute-start(bf16[7,3,64,64]{3,2,1,0:T(8,128)(2,1)S(1)} %pad_maximum_fusion.3), channel_id=1, source_target_pairs={{0,15},{1,0},{2,1},{3,2},{4,3},{5,4},{6,5},{7,6},{8,7},{9,8},{10,9... | collective-permute-start | bytes 516104 | tf_op jit(solution)/shard_map/ppermute | solution.py:18
  554.5 0.7 copy-start.2
  556.0 194.6 %collective-permute-start.7 = (bf16[7,3,64,64]{3,2,1,0:T(8,128)(2,1)}, bf16[7,3,64,64]{3,2,1,0:T(8,128)(2,1)}, u32[]{:S(2)}, u32[]{:S(2)}) collective-permute-start(bf16[7,3,64,64]{3,2,1,0:T(8,128)(2,1)} %pad_maximum_fusion.2), channel_id=1, source_target_pairs={{0,15},{1,0},{2,1},{3,2},{4,3},{5,4},{6,5},{7,6},{8,7},{9,8},{10,9... | collective-permute-start | bytes 516104 | tf_op jit(solution)/shard_map/ppermute | solution.py:18
  635.7 114.9 %copy-start.3 = (bf16[3,4,64,64]{3,2,1,0:T(8,128)(2,1)S(1)}, bf16[3,4,64,64]{3,2,1,0:T(8,128)(2,1)}, u32[]{:S(2)}) copy-start(bf16[3,4,64,64]{3,2,1,0:T(8,128)(2,1)} %copy-done.2) | copy-start | bytes 294916
  751.8 115.0 %copy-start.4 = (f32[64,512]{1,0:T(8,128)S(1)}, f32[64,512]{1,0:T(8,128)}, u32[]{:S(2)}) copy-start(f32[64,512]{1,0:T(8,128)} %fusion.161) | copy-start | bytes 393220
  866.7 9.0 %copy-start.1 = (f32[32,64]{1,0:T(8,128)S(1)}, f32[32,64]{1,0:T(8,128)}, u32[]{:S(2)}) copy-start(f32[32,64]{1,0:T(8,128)} %param.19) | copy-start | bytes 24580
where the time goes:
time: 884 us; the launch traced here: 876 us
  other arithmetic  386 us (44%)
  local copies, waits for them, and re-layouts  251 us (28%)
  blocking collectives  76.5 us (9%)
  starting transfers between devices  55.5 us (6%)
  matrix products  54.9 us (6%)
  waiting for transfers between devices  49.8 us (6%)
    scatter-add x2, other arithmetic, add_block(): return totals.at[cell_ids.reshape(-1)].add(products.reshape(-1, channels))  349 us
    gather x2, local copies, waits for them, and re-layouts, take_block(): flattened[cell_ids.reshape(-1)].reshape(64, block_len, channels)  230 us
    psum x1, blocking collectives, per_device(): filter_grad = lax.psum(partial_grad, ('slab', 'pencil'))  76.5 us
    dot_general x28, matrix products, contract(): jnp.einsum(pattern, operand, table_low, preferred_element_type=jnp.float32)  22.5 us
    dot_general x28, matrix products, contract(): jnp.einsum(pattern, operand, table_high, preferred_element_type=jnp.float32)  19.5 us
  transfers between devices with their start and end apart: 16, of which 10 were waited for; matrix products, arithmetic and copies ran while one was open for 39% of the time, Pallas kernels for 0%

commit v1 on v0

v1 whole, which is shorter than its diff:
```python
import jax
import jax.numpy as jnp
import numpy as np
from jax import lax
from jax.sharding import PartitionSpec as P

C = 64
NB = 32
ENV_SCALE = 40.0
ENV_WIDTH = 16.0


def wave_order(groups):
    count = 4 * groups
    rows = []
    for g in range(groups):
        rows += [2 * g, 2 * g + 1, count - 2 * g if g else count // 2, count - 1 - 2 * g]
    return np.array(rows)


def dft_table(waves, count, inverse):
    angles = (waves[:, None] * np.arange(count)[None, :] % count) * (2.0 * np.pi / count)
    cosines, sines = np.cos(angles), np.sin(angles)
    if inverse:
        return np.concatenate([cosines.T, -sines.T], axis=1) / count
    return np.concatenate([cosines, sines], axis=1)


def turned(values):
    return jnp.concatenate([values[..., C:], -values[..., :C]], axis=-1)


def transform(values, axis, table):
    table = jnp.asarray(table, jnp.bfloat16)
    doubled = jnp.concatenate([values, turned(values)], axis=axis)
    out = lax.dot_general(table, doubled, (((1,), (axis,)), ((), ())), preferred_element_type=jnp.float32)
    return jnp.moveaxis(out, 0, axis)


def spline_weights(frac):
    remain = 1.0 - frac
    square = frac * frac
    cubed = square * frac
    return [
        remain * remain * remain / 6.0,
        (3.0 * cubed - 6.0 * square + 4.0) / 6.0,
        (-3.0 * cubed + 3.0 * square + 3.0 * frac + 1.0) / 6.0,
        cubed / 6.0,
    ]


def placed(weights, first, length, wrap):
    cells = lax.broadcasted_iota(jnp.int32, (length, first.shape[0]), 0)
    gap = cells - first[None, :]
    if wrap:
        gap = jnp.where(gap < 0, gap + length, gap)
    out = jnp.zeros(gap.shape, jnp.float32)
    for j in range(4):
        out = jnp.where(gap == j, weights[j][None, :], out)
    return out


def passed_along(value, axis, steps):
    count = lax.axis_size(axis)
    return lax.ppermute(value, axis, [(s, (s + steps) % count) for s in range(count)])


def frequency(waves, count):
    return jnp.where(waves < count // 2, waves, waves - count).astype(jnp.float32)


def local_waves(index, count):
    l = jnp.arange(4, dtype=jnp.int32)
    out = jnp.where(l < 2, 2 * index + l, count - 2 * index - (l - 2))
    return jnp.where((l == 2) & (index == 0), count // 2, out)


def per_device(charges, cotangent, base_cell, frac, counts, filter_weights):
    groups = lax.axis_size("slab")
    n = 4 * groups
    si = lax.axis_index("slab")
    pi = lax.axis_index("pencil")
    slots = charges.shape[1]
    vals = jnp.concatenate([charges, cotangent], axis=0)
    live = (jnp.arange(slots, dtype=jnp.int32) < counts[0]).astype(jnp.float32)
    wx = placed(spline_weights(frac[0]), base_cell[0] - 4 * si, 7, False) * live[None, :]
    wy = placed(spline_weights(frac[1]), base_cell[1] - 4 * pi, 7, False)
    wz = placed(spline_weights(frac[2]), base_cell[2], n, True)
    stencil = (wx[:, None, None, :] * wy[None, :, None, :] * wz[None, None, :, :]).astype(jnp.bfloat16)
    stencil = stencil.reshape(49 * n, slots)
    density = lax.dot_general(stencil, vals, (((1,), (1,)), ((), ())), preferred_element_type=jnp.float32)
    density = density.reshape(7, 7, n, 2 * C)
    up = passed_along(density[:, 5:].astype(jnp.bfloat16), "pencil", 1).astype(jnp.float32)
    down = passed_along(density[:, :1].astype(jnp.bfloat16), "pencil", -1).astype(jnp.float32)
    density = density[:, 1:5].at[:, :2].add(up).at[:, 3:].add(down)
    up = passed_along(density[5:].astype(jnp.bfloat16), "slab", 1).astype(jnp.float32)
    down = passed_along(density[:1].astype(jnp.bfloat16), "slab", -1).astype(jnp.float32)
    density = density[1:5].at[:2].add(up).at[3:].add(down).astype(jnp.bfloat16)

    waves = wave_order(groups)
    ahead = dft_table(waves, n, False)
    behind = dft_table((-waves) % n, n, False)
    back = dft_table(waves, n, True)
    spec = transform(density, 2, ahead).astype(jnp.bfloat16)
    spec = lax.all_to_all(spec, "pencil", split_axis=2, concat_axis=1, tiled=True)
    spec = transform(spec, 1, ahead).astype(jnp.bfloat16)
    spec = lax.all_to_all(spec, "slab", split_axis=1, concat_axis=0, tiled=True)
    both = transform(spec, 0, np.concatenate([ahead, behind], axis=0))
    spec, mirror = both[:n], both[n:]

    ky, kz = local_waves(si, n), local_waves(pi, n)
    fx = frequency(jnp.asarray(waves, jnp.int32), n)
    fy, fz = frequency(ky, n), frequency(kz, n)
    kappa_sq = fx[:, None, None] ** 2 + fy[None, :, None] ** 2 + fz[None, None, :] ** 2
    kappa = jnp.sqrt(kappa_sq)
    spacing = n / (2.0 * NB)
    centers = (jnp.arange(NB, dtype=jnp.float32) + 0.5) * spacing
    envelope = ENV_SCALE * ENV_WIDTH / (ENV_WIDTH + kappa_sq)
    shells = envelope[..., None] * jnp.exp(-jnp.square((kappa[..., None] - centers) / spacing))
    shells = shells.reshape(n * 16, NB)
    profile = jnp.dot(shells, jnp.tile(filter_weights, (1, 2)), precision=lax.Precision.HIGHEST)
    profile = profile.reshape(n, 4, 4, 2 * C)

    def flipped(values, axis, index):
        a, b, c, d = [lax.index_in_dim(values, l, axis) for l in range(4)]
        first = index == 0
        return jnp.concatenate([jnp.where(first, a, c), d, jnp.where(first, c, a), b], axis=axis)

    mirror = flipped(flipped(mirror, 1, si), 2, pi)
    mirror = jnp.concatenate([mirror[..., C:], mirror[..., :C]], axis=-1)
    product = (spec * mirror).reshape(n * 16, 2 * C)
    partial = jnp.dot(shells.T, product[:, :C] + product[:, C:], precision=lax.Precision.HIGHEST)
    partial = partial * (0.5 / (n * n * n))
    part = lax.all_to_all(partial.reshape(groups, NB // groups, C), "slab", 0, 0, tiled=True).sum(axis=0)
    part = lax.all_gather(part, "pencil").sum(axis=0)
    grad = lax.all_gather(part, "slab").reshape(NB, C)

    field = (spec * profile).astype(jnp.bfloat16)
    field = transform(field, 0, back).astype(jnp.bfloat16)
    field = lax.all_to_all(field, "slab", split_axis=0, concat_axis=1, tiled=True)
    field = transform(field, 1, back).astype(jnp.bfloat16)
    field = lax.all_to_all(field, "pencil", split_axis=1, concat_axis=2, tiled=True)
    field = transform(field, 2, back).astype(jnp.bfloat16)
    low = passed_along(field[3:], "slab", 1)
    high = passed_along(field[:2], "slab", -1)
    field = jnp.concatenate([low, field, high], axis=0)
    low = passed_along(field[:, 3:], "pencil", 1)
    high = passed_along(field[:, :2], "pencil", -1)
    field = jnp.concatenate([low, field, high], axis=1).reshape(49 * n, 2 * C)
    out = lax.dot_general(field, stencil, (((0,), (0,)), ((), ())), preferred_element_type=jnp.float32)
    out = out.astype(jnp.bfloat16)
    return (out[:C], out[C:], grad)


def solution(mesh):
    spread = P(None, ("slab", "pencil"))
    return jax.shard_map(
        per_device,
        mesh=mesh,
        in_specs=(spread, spread, spread, spread, P(("slab", "pencil")), P()),
        out_specs=(spread, spread, P()),
        check_vma=False,
    )
```

time: 884 us -> 158 us (0.18)
  the two profiles are of different devices: /device:TPU:1 before, /device:TPU:32 now
where the time goes in v1:
time: 158 us; the launch traced here: 157 us
  blocking collectives  53.6 us (34%)
  waiting for transfers between devices  45.7 us (29%)
  starting transfers between devices  38.1 us (24%)
  local copies, waits for them, and re-layouts  7.44 us (5%)
  matrix products  6.01 us (4%)
  other arithmetic  4.19 us (3%)
  between operations  1.76 us (1%)
    all_gather x1, blocking collectives, per_device(): grad = lax.all_gather(part, 'slab').reshape(NB, C)  21.5 us
    all_gather x1, blocking collectives, per_device(): part = lax.all_gather(part, 'pencil').sum(axis=0)  17.5 us
    all_to_all x1, blocking collectives, per_device(): lax.all_to_all(partial.reshape(groups, NB // groups, C), 'slab', 0, 0, ti...  14.6 us
    ppermute x8, starting transfers between devices, passed_along(): lax.ppermute(value, axis, [(s, (s + steps) % count) for s in range(count)])  14.4 us
    ppermute x8, waiting for transfers between devices, passed_along(): lax.ppermute(value, axis, [(s, (s + steps) % count) for s in range(count)])  10.2 us
    all_to_all x1, waiting for transfers between devices, per_device(): lax.all_to_all(spec, 'pencil', split_axis=2, concat_axis=1, tiled=True)  9.37 us
    all_to_all x1, waiting for transfers between devices, per_device(): lax.all_to_all(field, 'pencil', split_axis=1, concat_axis=2, tiled=True)  9.36 us
    all_to_all x1, starting transfers between devices, per_device(): lax.all_to_all(spec, 'pencil', split_axis=2, concat_axis=1, tiled=True)  8.47 us
  transfers between devices with their start and end apart: 12, of which 8 were waited for; matrix products, arithmetic and copies ran while one was open for 3% of the time, Pallas kernels for 0%

profile of v1, /device:TPU:32, one launch (start us, length us, event | category | flops | bytes accessed | tf_op | source)
XLA Modules:
  0.0 156.8 jit_solution(6255527720152603941)
XLA Ops:
  1.3 0.8 broadcast_multiply_fusion.3
  2.1 0.8 slice_subtract_fusion.1
  3.1 1.9 %fusion.115 = (bf16[7,7,64,128]{3,2,1,0:T(8,128)(2,1)S(1)}, f32[7,7,64,128]{3,2,1,0:T(8,128)S(1)}) fusion(bf16[64,512]{1,0:T(8,128)(2,1)} %param.22, bf16[64,512]{1,0:T(8,128)(2,1)} %param.21, f32[64,512]{1,0:T(8,128)S(1)} %select_select_fusion, f32[7,7,512]{2,1,0:T(8,128)S(1)} %broadcast_multiply_fusion), kind=kOutput, calls=%fused_computation.181 | convolution fusion | flops 414916608 | bytes 2770944 | tf_op jit(solution)/shard_map/dot_general | solution.py:91
  5.0 1.7 %collective-permute-start.1 = (bf16[7,1,64,128]{3,2,1,0:T(8,128)(2,1)S(1)}, bf16[7,1,64,128]{3,2,1,0:T(8,128)(2,1)S(1)}, u32[]{:S(2)}, u32[]{:S(2)}) collective-permute-start(bf16[7,1,64,128]{3,2,1,0:T(8,128)(2,1)S(1)} %slice.310), channel_id=1, source_target_pairs={{0,15},{1,0},{2,1},{3,2},{4,3},{5,4},{6,5},{7,6},{8,7},{9,8},{10,9... | collective-permute-start | bytes 344072 | tf_op jit(solution)/shard_map/ppermute | solution.py:65
  6.8 0.1 slice.306
  6.8 3.6 %collective-permute-done = bf16[7,2,64,128]{3,2,1,0:T(8,128)(2,1)S(1)} collective-permute-done((bf16[7,2,64,128]{3,2,1,0:T(8,128)(2,1)S(1)}, bf16[7,2,64,128]{3,2,1,0:T(8,128)(2,1)S(1)}, u32[]{:S(2)}, u32[]{:S(2)}) %collective-permute-start) | collective-permute-done | bytes 229408 | tf_op jit(solution)/shard_map/ppermute | solution.py:65
  10.7 1.7 %collective-permute-start.2 = (bf16[2,4,64,128]{3,2,1,0:T(8,128)(2,1)S(1)}, bf16[2,4,64,128]{3,2,1,0:T(8,128)(2,1)S(1)}, u32[]{:S(2)}, u32[]{:S(2)}) collective-permute-start(bf16[2,4,64,128]{3,2,1,0:T(8,128)(2,1)S(1)} %slice.313), channel_id=1, source_target_pairs={{0,16},{16,32},{32,48},{48,64},{64,80},{80,96},{96,112},{112,128},... | collective-permute-start | bytes 393224 | tf_op jit(solution)/shard_map/ppermute | solution.py:65
  12.4 3.8 %collective-permute-start.3 = (bf16[1,4,64,128]{3,2,1,0:T(8,128)(2,1)S(1)}, bf16[1,4,64,128]{3,2,1,0:T(8,128)(2,1)S(1)}, u32[]{:S(2)}, u32[]{:S(2)}) collective-permute-start(bf16[1,4,64,128]{3,2,1,0:T(8,128)(2,1)S(1)} %slice.315), channel_id=1, source_target_pairs={{0,240},{16,0},{32,16},{48,32},{64,48},{80,64},{96,80},{112,96},{1... | collective-permute-start | bytes 196616 | tf_op jit(solution)/shard_map/ppermute | solution.py:65
  16.2 4.1 %collective-permute-done.2 = bf16[2,4,64,128]{3,2,1,0:T(8,128)(2,1)S(1)} collective-permute-done((bf16[2,4,64,128]{3,2,1,0:T(8,128)(2,1)S(1)}, bf16[2,4,64,128]{3,2,1,0:T(8,128)(2,1)S(1)}, u32[]{:S(2)}, u32[]{:S(2)}) %collective-permute-start.2) | collective-permute-done | bytes 131104 | tf_op jit(solution)/shard_map/ppermute | solution.py:65
  20.5 0.1 fusion.113
  20.7 0.3 fusion.7
  21.0 0.9 copy.38
  21.9 8.5 %all-to-all-start = ((bf16[4,4,64,128]{3,1,0,2:T(4,128)(2,1)}), bf16[4,4,64,128]{3,1,0,2:T(4,128)(2,1)S(1)}, u32[]{:S(2)}, u32[]{:S(2)}) async-start(bf16[4,4,64,128]{3,1,0,2:T(4,128)(2,1)} %copy.38), calls=%async_computation | async-start | bytes 524288 | tf_op jit(solution)/shard_map/all_to_all | solution.py:105
  30.4 0.1 reshape.575
  30.5 0.1 broadcast_add_fusion
  30.6 9.4 %all-to-all-done = bf16[4,4,64,128]{3,1,0,2:T(4,128)(2,1)S(1)} async-done(((bf16[4,4,64,128]{3,1,0,2:T(4,128)(2,1)}), bf16[4,4,64,128]{3,1,0,2:T(4,128)(2,1)S(1)}, u32[]{:S(2)}, u32[]{:S(2)}) %all-to-all-start) | async-done | bytes 262176 | tf_op jit(solution)/shard_map/all_to_all | solution.py:105
  39.9 0.1 copy.39
  40.1 0.1 fusion.112
  40.2 0.3 fusion.8
  40.5 0.9 copy.40
  41.4 6.1 %all-to-all-start.1 = ((bf16[4,64,4,128]{3,2,0,1:T(4,128)(2,1)}), bf16[4,64,4,128]{3,2,0,1:T(4,128)(2,1)S(1)}, u32[]{:S(2)}, u32[]{:S(2)}) async-start(bf16[4,64,4,128]{3,2,0,1:T(4,128)(2,1)} %copy.40), calls=%async_computation.1 | async-start | bytes 524288 | tf_op jit(solution)/shard_map/all_to_all | solution.py:107
  47.5 0.1 fusion.90
  47.6 0.1 copy.46
  47.7 0.2 div.78
  47.9 0.1 copy.47
  48.0 0.2 sqrt.12
  48.2 8.4 %all-to-all-done.1 = bf16[4,64,4,128]{3,2,0,1:T(4,128)(2,1)S(1)} async-done(((bf16[4,64,4,128]{3,2,0,1:T(4,128)(2,1)}), bf16[4,64,4,128]{3,2,0,1:T(4,128)(2,1)S(1)}, u32[]{:S(2)}, u32[]{:S(2)}) %all-to-all-start.1) | async-done | bytes 262176 | tf_op jit(solution)/shard_map/all_to_all | solution.py:107
  56.6 0.1 copy.41
  56.7 0.1 fusion.111
  56.9 0.4 fusion.34
  57.2 1.1 fusion.6
  58.3 0.1 fusion.110
  58.5 0.3 fusion.9
  58.8 0.9 copy.42
  59.7 3.6 %all-to-all-start.2 = ((bf16[64,4,4,128]{3,2,1,0:T(4,128)(2,1)}), bf16[64,4,4,128]{3,2,1,0:T(4,128)(2,1)S(1)}, u32[]{:S(2)}, u32[]{:S(2)}) async-start(bf16[64,4,4,128]{3,2,1,0:T(4,128)(2,1)} %copy.42), calls=%async_computation.2 | async-start | bytes 524288 | tf_op jit(solution)/shard_map/all_to_all | solution.py:140
  63.4 8.4 %all-to-all-done.2 = bf16[64,4,4,128]{3,2,1,0:T(4,128)(2,1)S(1)} async-done(((bf16[64,4,4,128]{3,2,1,0:T(4,128)(2,1)}), bf16[64,4,4,128]{3,2,1,0:T(4,128)(2,1)S(1)}, u32[]{:S(2)}, u32[]{:S(2)}) %all-to-all-start.2) | async-done | bytes 262176 | tf_op jit(solution)/shard_map/all_to_all | solution.py:140
  71.8 0.1 copy.43
  71.9 0.1 fusion.109
  72.1 0.3 fusion.10
  72.4 0.9 copy.44
  73.3 5.4 %all-to-all-start.3 = ((bf16[4,64,4,128]{3,2,0,1:T(4,128)(2,1)}), bf16[4,64,4,128]{3,2,0,1:T(4,128)(2,1)S(1)}, u32[]{:S(2)}, u32[]{:S(2)}) async-start(bf16[4,64,4,128]{3,2,0,1:T(4,128)(2,1)} %copy.44), calls=%async_computation.3 | async-start | bytes 524288 | tf_op jit(solution)/shard_map/all_to_all | solution.py:142
  78.8 0.2 fusion.107
  79.0 9.4 %all-to-all-done.3 = bf16[4,64,4,128]{3,2,0,1:T(4,128)(2,1)S(1)} async-done(((bf16[4,64,4,128]{3,2,0,1:T(4,128)(2,1)}), bf16[4,64,4,128]{3,2,0,1:T(4,128)(2,1)S(1)}, u32[]{:S(2)}, u32[]{:S(2)}) %all-to-all-start.3) | async-done | bytes 262176 | tf_op jit(solution)/shard_map/all_to_all | solution.py:142
  88.4 0.1 copy.45
  88.5 0.1 fusion.108
  88.7 0.3 fusion.11
  89.0 0.5 collective-permute-start.4
  89.5 5.0 %collective-permute-start.5 = (bf16[2,4,64,128]{3,2,1,0:T(8,128)(2,1)S(1)}, bf16[2,4,64,128]{3,2,1,0:T(8,128)(2,1)S(1)}, u32[]{:S(2)}, u32[]{:S(2)}) collective-permute-start(bf16[2,4,64,128]{3,2,1,0:T(8,128)(2,1)S(1)} %slice.330), channel_id=1, source_target_pairs={{0,240},{16,0},{32,16},{48,32},{64,48},{80,64},{96,80},{112,96},{1... | collective-permute-start | bytes 393224 | tf_op jit(solution)/shard_map/ppermute | solution.py:65
  94.4 0.2 maximum_multiply_fusion
  94.6 0.3 copy.48
  95.0 1.8 %collective-permute-done.4 = bf16[1,4,64,128]{3,2,1,0:T(8,128)(2,1)S(1)} collective-permute-done((bf16[1,4,64,128]{3,2,1,0:T(8,128)(2,1)S(1)}, bf16[1,4,64,128]{3,2,1,0:T(8,128)(2,1)S(1)}, u32[]{:S(2)}, u32[]{:S(2)}) %collective-permute-start.4) | collective-permute-done | bytes 65568 | tf_op jit(solution)/shard_map/ppermute | solution.py:65
  96.8 0.7 collective-permute-done.5
  97.5 1.7 %collective-permute-start.7 = (bf16[7,2,64,128]{3,2,1,0:T(8,128)(2,1)S(1)}, bf16[7,2,64,128]{3,2,1,0:T(8,128)(2,1)S(1)}, u32[]{:S(2)}, u32[]{:S(2)}) collective-permute-start(bf16[7,2,64,128]{3,2,1,0:T(8,128)(2,1)S(1)} %pad_maximum_fusion.2), channel_id=1, source_target_pairs={{0,15},{1,0},{2,1},{3,2},{4,3},{5,4},{6,5},{7,6},{8,7},{9,8},{10,9... | collective-permute-start | bytes 688136 | tf_op jit(solution)/shard_map/ppermute | solution.py:65
  99.3 0.5 convolution_multiply_fusion.1
  99.8 0.1 reshape.579
  99.9 14.6 %all_to_all.77 = f32[16,1,128]{2,1,0:T(1,128)S(1)} all-to-all(f32[16,1,128]{2,1,0:T(1,128)S(1)} %reshape.579), channel_id=1, replica_groups=mesh['slab'=16,'pencil'=16] {'slab'}, dimensions={0} | all-to-all | bytes 16384 | tf_op jit(solution)/shard_map/all_to_all | solution.py:134
  114.5 0.5 broadcast.645
  115.0 0.7 reduce.9
  115.6 0.1 reshape.580
  115.8 17.5 %all-gather.2 = f32[16,2,64]{2,1,0:T(2,128)S(1)} all-gather(f32[1,2,64]{2,1,0:T(2,128)S(1)} %bitcast.110), channel_id=2, replica_groups=mesh['slab'=16,'pencil'=16] {'pencil'}, dimensions={0}, use_global_device_ids=true | all-gather | bytes 8704 | tf_op jit(solution)/shard_map/all_gather | solution.py:135
  133.3 21.5 %all-gather.3 = f32[16,2,64]{2,1,0:T(2,128)S(1)} all-gather(f32[1,2,64]{2,1,0:T(2,128)S(1)} %bitcast.109), channel_id=3, replica_groups=mesh['slab'=16,'pencil'=16] {'slab'}, dimensions={0}, use_global_device_ids=true | all-gather | bytes 8704 | tf_op jit(solution)/shard_map/all_gather | solution.py:136
  154.8 0.7 fusion.13
  155.5 0.7 fusion.114
  156.2 0.6 copy.61
  (45 shorter events, 0.9 us)
Async XLA Ops:
  5.0 5.5 %collective-permute-start = (bf16[7,2,64,128]{3,2,1,0:T(8,128)(2,1)S(1)}, bf16[7,2,64,128]{3,2,1,0:T(8,128)(2,1)S(1)}, u32[]{:S(2)}, u32[]{:S(2)}) collective-permute-start(bf16[7,2,64,128]{3,2,1,0:T(8,128)(2,1)S(1)} %slice.308), channel_id=1, source_target_pairs={{0,1},{1,2},{2,3},{3,4},{4,5},{5,6},{6,7},{7,8},{8,9},{9,10},{10,1... | collective-permute-start | bytes 688136 | tf_op jit(solution)/shard_map/ppermute | solution.py:65
  5.0 5.5 %collective-permute-start.1 = (bf16[7,1,64,128]{3,2,1,0:T(8,128)(2,1)S(1)}, bf16[7,1,64,128]{3,2,1,0:T(8,128)(2,1)S(1)}, u32[]{:S(2)}, u32[]{:S(2)}) collective-permute-start(bf16[7,1,64,128]{3,2,1,0:T(8,128)(2,1)S(1)} %slice.310), channel_id=1, source_target_pairs={{0,15},{1,0},{2,1},{3,2},{4,3},{5,4},{6,5},{7,6},{8,7},{9,8},{10,9... | collective-permute-start | bytes 344072 | tf_op jit(solution)/shard_map/ppermute | solution.py:65
  10.7 9.7 %collective-permute-start.2 = (bf16[2,4,64,128]{3,2,1,0:T(8,128)(2,1)S(1)}, bf16[2,4,64,128]{3,2,1,0:T(8,128)(2,1)S(1)}, u32[]{:S(2)}, u32[]{:S(2)}) collective-permute-start(bf16[2,4,64,128]{3,2,1,0:T(8,128)(2,1)S(1)} %slice.313), channel_id=1, source_target_pairs={{0,16},{16,32},{32,48},{48,64},{64,80},{80,96},{96,112},{112,128},... | collective-permute-start | bytes 393224 | tf_op jit(solution)/shard_map/ppermute | solution.py:65
  12.4 8.3 %copy-start.4 = (bf16[64,128,1,1]{1,0,3,2:T(8,128)(2,1)S(1)}, bf16[64,128,1,1]{1,0,3,2:T(8,128)(2,1)}, u32[]{:S(2)}) copy-start(bf16[64,128,1,1]{1,0,3,2:T(8,128)(2,1)} %constant.198) | copy-start | bytes 49156
  12.4 8.0 %collective-permute-start.3 = (bf16[1,4,64,128]{3,2,1,0:T(8,128)(2,1)S(1)}, bf16[1,4,64,128]{3,2,1,0:T(8,128)(2,1)S(1)}, u32[]{:S(2)}, u32[]{:S(2)}) collective-permute-start(bf16[1,4,64,128]{3,2,1,0:T(8,128)(2,1)S(1)} %slice.315), channel_id=1, source_target_pairs={{0,240},{16,0},{32,16},{48,32},{64,48},{80,64},{96,80},{112,96},{1... | collective-permute-start | bytes 196616 | tf_op jit(solution)/shard_map/ppermute | solution.py:65
  20.5 9.8 %copy-start.1 = (f32[32,64]{1,0:T(8,128)S(1)}, f32[32,64]{1,0:T(8,128)}, u32[]{:S(2)}) copy-start(f32[32,64]{1,0:T(8,128)} %param.26) | copy-start | bytes 24580
  20.5 10.0 %copy-start.2 = (f32[64]{0:T(128)S(1)}, f32[64]{0:T(128)}, u32[]{:S(2)}) copy-start(f32[64]{0:T(128)} %constant.196) | copy-start | bytes 772
  21.9 18.1 %all-to-all-start = ((bf16[4,4,64,128]{3,1,0,2:T(4,128)(2,1)}), bf16[4,4,64,128]{3,1,0,2:T(4,128)(2,1)S(1)}, u32[]{:S(2)}, u32[]{:S(2)}) async-start(bf16[4,4,64,128]{3,1,0,2:T(4,128)(2,1)} %copy.38), calls=%async_computation | async-start | bytes 524288 | tf_op jit(solution)/shard_map/all_to_all | solution.py:105
  40.5 16.3 %copy-start = (bf16[128,128,1,1]{1,0,3,2:T(8,128)(2,1)S(1)}, bf16[128,128,1,1]{1,0,3,2:T(8,128)(2,1)}, u32[]{:S(2)}) copy-start(bf16[128,128,1,1]{1,0,3,2:T(8,128)(2,1)} %constant.197) | copy-start | bytes 98308
  41.4 15.2 %all-to-all-start.1 = ((bf16[4,64,4,128]{3,2,0,1:T(4,128)(2,1)}), bf16[4,64,4,128]{3,2,0,1:T(4,128)(2,1)S(1)}, u32[]{:S(2)}, u32[]{:S(2)}) async-start(bf16[4,64,4,128]{3,2,0,1:T(4,128)(2,1)} %copy.40), calls=%async_computation.1 | async-start | bytes 524288 | tf_op jit(solution)/shard_map/all_to_all | solution.py:107
  56.8 1.6 %copy-start.3 = (bf16[64,128,1,1]{1,0,3,2:T(8,128)(2,1)S(1)}, bf16[64,128,1,1]{1,0,3,2:T(8,128)(2,1)}, u32[]{:S(2)}) copy-start(bf16[64,128,1,1]{1,0,3,2:T(8,128)(2,1)} %constant.199) | copy-start | bytes 49156
  59.7 12.1 %all-to-all-start.2 = ((bf16[64,4,4,128]{3,2,1,0:T(4,128)(2,1)}), bf16[64,4,4,128]{3,2,1,0:T(4,128)(2,1)S(1)}, u32[]{:S(2)}, u32[]{:S(2)}) async-start(bf16[64,4,4,128]{3,2,1,0:T(4,128)(2,1)} %copy.42), calls=%async_computation.2 | async-start | bytes 524288 | tf_op jit(solution)/shard_map/all_to_all | solution.py:140
  73.3 15.1 %all-to-all-start.3 = ((bf16[4,64,4,128]{3,2,0,1:T(4,128)(2,1)}), bf16[4,64,4,128]{3,2,0,1:T(4,128)(2,1)S(1)}, u32[]{:S(2)}, u32[]{:S(2)}) async-start(bf16[4,64,4,128]{3,2,0,1:T(4,128)(2,1)} %copy.44), calls=%async_computation.3 | async-start | bytes 524288 | tf_op jit(solution)/shard_map/all_to_all | solution.py:142
  89.0 7.8 %collective-permute-start.4 = (bf16[1,4,64,128]{3,2,1,0:T(8,128)(2,1)S(1)}, bf16[1,4,64,128]{3,2,1,0:T(8,128)(2,1)S(1)}, u32[]{:S(2)}, u32[]{:S(2)}) collective-permute-start(bf16[1,4,64,128]{3,2,1,0:T(8,128)(2,1)S(1)} %slice.329), channel_id=1, source_target_pairs={{0,16},{16,32},{32,48},{48,64},{64,80},{80,96},{96,112},{112,128},... | collective-permute-start | bytes 196616 | tf_op jit(solution)/shard_map/ppermute | solution.py:65
  89.5 8.0 %collective-permute-start.5 = (bf16[2,4,64,128]{3,2,1,0:T(8,128)(2,1)S(1)}, bf16[2,4,64,128]{3,2,1,0:T(8,128)(2,1)S(1)}, u32[]{:S(2)}, u32[]{:S(2)}) collective-permute-start(bf16[2,4,64,128]{3,2,1,0:T(8,128)(2,1)S(1)} %slice.330), channel_id=1, source_target_pairs={{0,240},{16,0},{32,16},{48,32},{64,48},{80,64},{96,80},{112,96},{1... | collective-permute-start | bytes 393224 | tf_op jit(solution)/shard_map/ppermute | solution.py:65
  97.5 57.3 %collective-permute-start.6 = (bf16[7,1,64,128]{3,2,1,0:T(8,128)(2,1)S(1)}, bf16[7,1,64,128]{3,2,1,0:T(8,128)(2,1)S(1)}, u32[]{:S(2)}, u32[]{:S(2)}) collective-permute-start(bf16[7,1,64,128]{3,2,1,0:T(8,128)(2,1)S(1)} %pad_maximum_fusion.4), channel_id=1, source_target_pairs={{0,1},{1,2},{2,3},{3,4},{4,5},{5,6},{6,7},{7,8},{8,9},{9,10},{10,1... | collective-permute-start | bytes 344072 | tf_op jit(solution)/shard_map/ppermute | solution.py:65
  97.5 57.3 %collective-permute-start.7 = (bf16[7,2,64,128]{3,2,1,0:T(8,128)(2,1)S(1)}, bf16[7,2,64,128]{3,2,1,0:T(8,128)(2,1)S(1)}, u32[]{:S(2)}, u32[]{:S(2)}) collective-permute-start(bf16[7,2,64,128]{3,2,1,0:T(8,128)(2,1)S(1)} %pad_maximum_fusion.2), channel_id=1, source_target_pairs={{0,15},{1,0},{2,1},{3,2},{4,3},{5,4},{6,5},{7,6},{8,7},{9,8},{10,9... | collective-permute-start | bytes 688136 | tf_op jit(solution)/shard_map/ppermute | solution.py:65

commit v2 on v1

v2 whole, which is shorter than its diff:
```python
import functools

import jax
import jax.numpy as jnp
import numpy as np
from jax import lax
from jax.experimental import pallas as pl
from jax.experimental.pallas import tpu as pltpu
from jax.sharding import PartitionSpec as P

C = 64
L = 2 * C
NB = 32
ENV_SCALE = 40.0
ENV_WIDTH = 16.0
MESH = pl.DeviceIdType.MESH
F32 = jnp.float32
BF16 = jnp.bfloat16


def wave_order(groups):
    count = 4 * groups
    rows = []
    for g in range(groups):
        rows += [2 * g, 2 * g + 1, count - 2 * g if g else count // 2, count - 1 - 2 * g]
    return np.array(rows)


def tables(groups):
    count = 4 * groups
    waves = wave_order(groups)
    eye = np.eye(4)

    def parts(rows, inverse):
        angles = (rows[:, None] * np.arange(count)[None, :] % count) * (2.0 * np.pi / count)
        cosines, sines = np.cos(angles), np.sin(angles)
        return (cosines.T / count, -sines.T / count) if inverse else (cosines, sines)

    def joined(pair, pattern=None):
        size = 4 * count
        if pattern is not None:
            split = [t.reshape(groups, 4, groups, 4) for t in pair]
            pair = [np.einsum(pattern, t, eye).reshape(size, size) for t in split]
        return jnp.asarray(np.concatenate(pair, axis=1), BF16)

    ahead, back = parts(waves, False), parts(waves, True)
    mirror = parts((-waves) % count, False)
    z_ahead = joined(ahead, "glhm,yv->gylvhm")
    y_ahead = joined(ahead, "glhm,ab->glahmb")
    x_ahead = jnp.concatenate([joined(ahead), joined(mirror)], axis=0)
    x_back = joined(back)
    y_back = joined(back, "glhm,ab->glahmb")
    z_back = joined(back, "glhm,yv->yglhvm")
    return z_ahead, y_ahead, x_ahead, x_back, y_back, z_back


def spline_weights(frac):
    remain = 1.0 - frac
    square = frac * frac
    cubed = square * frac
    return [
        remain * remain * remain / 6.0,
        (3.0 * cubed - 6.0 * square + 4.0) / 6.0,
        (-3.0 * cubed + 3.0 * square + 3.0 * frac + 1.0) / 6.0,
        cubed / 6.0,
    ]


def placed(gap, weights):
    out = jnp.zeros(gap.shape, F32)
    for j in range(4):
        out = jnp.where(gap == j, weights[j], out)
    return out


def squared_wave(group, inner, count):
    wave = jnp.where(inner < 2, 2 * group + inner, count - 2 * group - inner + 2)
    wave = jnp.where((inner == 2) & (group == 0), count // 2, wave)
    wave = jnp.where(wave < count // 2, wave, wave - count)
    return wave * wave


def kernel(
    groups, count_ref, charges_ref, cot_ref, base_ref, frac_ref, weights_ref,
    za_ref, ya_ref, xa_ref, xb_ref, yb_ref, zb_ref,
    pot_ref, cg_ref, grad_ref,
    wx_ref, wy_ref, wz_ref, st_ref, vals_ref, den_ref, ys_ref, yu_ref, yd_ref, xs_ref, xu_ref, xd_ref,
    send_ref, recv_ref, line_ref, spec_ref, mirror_ref, prof_ref, shell_ref, corr_ref, field_ref, acc_ref,
    g1s_ref, g1r_ref, g2s_ref, g2r_ref, g3s_ref, g3r_ref,
    hs, hr, es, er, local_sem,
):
    G = groups
    N = 4 * G
    R = 4 * N
    si = lax.axis_index("slab")
    pi = lax.axis_index("pencil")
    where_is = {"slab": si, "pencil": pi}
    slots = charges_ref.shape[1]

    barrier = pltpu.get_barrier_semaphore()

    def greet(d, carry):
        pl.semaphore_signal(barrier, inc=1, device_id={"slab": lax.rem(si + d, G)}, device_id_type=MESH)
        pl.semaphore_signal(barrier, inc=1, device_id={"pencil": lax.rem(pi + d, G)}, device_id_type=MESH)
        return carry

    lax.fori_loop(1, G, greet, 0)

    def shift(i, src, dst, axis, step):
        peer = lax.rem(where_is[axis] + step + G, G)
        return pltpu.make_async_remote_copy(
            src_ref=src, dst_ref=dst, send_sem=hs.at[i], recv_sem=hr.at[i],
            device_id={axis: peer}, device_id_type=MESH,
        )

    def hop(phase, src_of, dst, axis, d, to_peer):
        me = where_is[axis]
        peer = lax.rem(me + d, G)
        landed = me if to_peer else lax.rem(me + G - d, G)
        return pltpu.make_async_remote_copy(
            src_ref=src_of(peer), dst_ref=dst.at[landed], send_sem=es.at[phase, d], recv_sem=er.at[phase, d],
            device_id={axis: peer}, device_id_type=MESH,
        )

    def exchange(phase, src_of, dst, axis):
        def start(d, carry):
            hop(phase, src_of, dst, axis, d, True).start()
            return carry

        lax.fori_loop(1, G, start, 0)

    def arrived(phase, src_of, dst, axis):
        def wait(d, carry):
            hop(phase, src_of, dst, axis, d, False).wait_recv()
            return carry

        lax.fori_loop(1, G, wait, 0)

    def drained(phase, src_of, dst, axis):
        def wait(d, carry):
            hop(phase, src_of, dst, axis, d, True).wait_send()
            return carry

        lax.fori_loop(1, G, wait, 0)

    lane = lax.broadcasted_iota(jnp.int32, (1, L), 1)
    sign = jnp.where(lane < C, 1.0, -1.0).astype(F32)

    def stage(table_ref, pieces):
        columns = []
        for piece in pieces:
            wide = piece.astype(F32)
            turned = (pltpu.roll(wide, C, 1) * sign).astype(BF16)
            columns.append(jnp.concatenate([piece.astype(BF16), turned], axis=0))
        out = jnp.dot(table_ref[...], jnp.concatenate(columns, axis=1), preferred_element_type=F32)
        return [out[:, i * L:(i + 1) * L] for i in range(len(pieces))]

    live = lax.broadcasted_iota(jnp.int32, (1, slots), 1) < count_ref[0]
    row = lax.broadcasted_iota(jnp.int32, (8, slots), 0)
    cell = jnp.where(row < 6, row + 1, jnp.where(row == 6, 0, -8))
    wx = placed(cell - (base_ref[0:1, :] - 4 * si), spline_weights(frac_ref[0:1, :]))
    wx_ref[...] = jnp.where(live, wx, 0.0)
    wy_ref[...] = placed(cell - (base_ref[1:2, :] - 4 * pi), spline_weights(frac_ref[1:2, :]))
    gap = lax.broadcasted_iota(jnp.int32, (N, slots), 0) - base_ref[2:3, :]
    wz_ref[...] = placed(jnp.where(gap < 0, gap + N, gap), spline_weights(frac_ref[2:3, :]))
    vals_ref[...] = jnp.concatenate([charges_ref[...], cot_ref[...]], axis=0).T

    def spread(x, first, last):
        along_x = wx_ref[pl.ds(x, 1), :]
        for y in range(first, last):
            st_ref[x, y] = (wz_ref[...] * (along_x * wy_ref[y:y + 1, :])).astype(BF16)
        left = st_ref[x, first:last].reshape((last - first) * N, slots)
        return jnp.dot(left, vals_ref[...], preferred_element_type=F32)

    def rim_block(x, carry):
        ys_ref[x] = spread(x, 4, 7).astype(BF16).reshape(3, N, L)
        return carry

    def own_block(x, carry):
        den_ref[x] = spread(x, 0, 4).reshape(4, N, L)
        return carry

    lax.fori_loop(0, 7, rim_block, 0)
    pl.semaphore_wait(barrier, 2 * (G - 1))
    y_rims = [
        shift(0, ys_ref.at[4:7, 0:2], yu_ref.at[4:7], "pencil", 1),
        shift(1, ys_ref.at[4:7, 2:3], yd_ref.at[4:7], "pencil", -1),
        shift(2, ys_ref.at[0:4, 0:2], yu_ref.at[0:4], "pencil", 1),
        shift(3, ys_ref.at[0:4, 2:3], yd_ref.at[0:4], "pencil", -1),
    ]
    for copy in y_rims:
        copy.start()
    lax.fori_loop(0, 7, own_block, 0)

    y_rims[0].wait_recv()
    y_rims[1].wait_recv()
    for x in range(4, 7):
        xs_ref[x - 4, 0:2] = (den_ref[x, 0:2] + yu_ref[x].astype(F32)).astype(BF16)
        xs_ref[x - 4, 2:3] = den_ref[x, 2:3].astype(BF16)
        xs_ref[x - 4, 3:4] = (den_ref[x, 3:4] + yd_ref[x].astype(F32)).astype(BF16)
    x_rims = [
        shift(4, xs_ref.at[0:2], xu_ref, "slab", 1),
        shift(5, xs_ref.at[2:3], xd_ref, "slab", -1),
    ]
    for copy in x_rims:
        copy.start()
    y_rims[2].wait_recv()
    y_rims[3].wait_recv()
    for x in range(4):
        den_ref[x, 0:2] += yu_ref[x].astype(F32)
        den_ref[x, 3:4] += yd_ref[x].astype(F32)
    x_rims[0].wait_recv()
    x_rims[1].wait_recv()
    for x in range(2):
        den_ref[x] += xu_ref[x].astype(F32)
    den_ref[3] += xd_ref[0].astype(F32)

    def both_ways(phase, axis):
        return lambda peer: send_ref.at[phase, peer], recv_ref.at[phase], axis

    def run_stage(phase, table_ref, pieces_of):
        for x in range(0, 4, 2):
            for i, out in enumerate(stage(table_ref, [pieces_of(x), pieces_of(x + 1)])):
                send_ref[phase, :, x + i] = out.astype(BF16).reshape(G, 16, L)

    def begin(phase, axis):
        me = where_is[axis]
        exchange(phase, *both_ways(phase, axis))
        pltpu.make_async_copy(send_ref.at[phase, me], recv_ref.at[phase, me], local_sem.at[phase]).start()

    def finish(phase, axis):
        me = where_is[axis]
        arrived(phase, *both_ways(phase, axis))
        pltpu.make_async_copy(send_ref.at[phase, me], recv_ref.at[phase, me], local_sem.at[phase]).wait()

    run_stage(0, za_ref, lambda x: den_ref[x].reshape(R, L))
    begin(0, "pencil")

    at = lax.broadcasted_iota(jnp.int32, (NB, 16 * N), 1)
    block = at // N
    along = at % N
    kappa_sq = (
        squared_wave(along // 4, along % 4, N)
        + squared_wave(si, block // 4, N)
        + squared_wave(pi, block % 4, N)
    ).astype(F32)
    spacing = N / (2.0 * NB)
    centers = (lax.broadcasted_iota(jnp.int32, (NB, 16 * N), 0).astype(F32) + 0.5) * spacing
    reach = (jnp.sqrt(kappa_sq) - centers) / spacing
    shell_ref[...] = ENV_SCALE * ENV_WIDTH / (ENV_WIDTH + kappa_sq) * jnp.exp(-(reach * reach))
    doubled = jnp.concatenate([weights_ref[...], weights_ref[...]], axis=1)
    prof_ref[...] = lax.dot_general(
        shell_ref[...], doubled, (((0,), (0,)), ((), ())),
        precision=lax.Precision.HIGHEST, preferred_element_type=F32,
    ).reshape(16, N, L)

    finish(0, "pencil")
    run_stage(1, ya_ref, lambda x: recv_ref[0, :, x].reshape(R, L))
    begin(1, "slab")
    finish(1, "slab")

    line_ref[...] = recv_ref[1].reshape(16 * N, L).astype(F32)
    for b in range(0, 16, 2):
        lines = [line_ref[pl.ds(b + i, N, stride=16), :] for i in range(2)]
        outs = stage(xa_ref, lines)
        for i in range(2):
            spec_ref[b + i] = outs[i][:N]
            mirror_ref[b + i] = outs[i][N:]
    for b in range(0, 16, 2):
        outs = stage(xb_ref, [spec_ref[b + i] * prof_ref[b + i] for i in range(2)])
        for i in range(2):
            line_ref[pl.ds(b + i, N, stride=16), :] = outs[i]
    send_ref[2] = line_ref[...].astype(BF16).reshape(G, 4, 16, L)
    begin(2, "slab")

    for b in range(16):
        j, l = b // 4, b % 4
        jm = jnp.where(si == 0, (4 - j) % 4, (j + 2) % 4)
        lm = jnp.where(pi == 0, (4 - l) % 4, (l + 2) % 4)
        opposite = mirror_ref[jm * 4 + lm]
        corr_ref[pl.ds(b * N, N), :] = spec_ref[b] * pltpu.roll(opposite, C, 1)
    partial = jnp.dot(
        shell_ref[...], corr_ref[...], precision=lax.Precision.HIGHEST, preferred_element_type=F32
    )
    partial = (partial + pltpu.roll(partial, C, 1)) * (0.5 / (N * N * N))
    rows = NB // G
    g1s_ref[...] = jnp.zeros_like(g1s_ref)
    for g in range(G):
        g1s_ref[g, 0:rows, :] = partial[g * rows:(g + 1) * rows]
    first = (lambda peer: g1s_ref.at[peer], g1r_ref, "slab")
    second = (lambda peer: g2s_ref, g2r_ref, "pencil")
    third = (lambda peer: g3s_ref, g3r_ref, "slab")
    exchange(4, *first)
    g1r_ref[pl.ds(si, 1)] = g1s_ref[pl.ds(si, 1)]

    finish(2, "slab")
    run_stage(3, yb_ref, lambda x: recv_ref[2, :, x].reshape(R, L))
    begin(3, "pencil")

    arrived(4, *first)
    total = jnp.sum(g1r_ref[...], axis=0)
    g2s_ref[...] = total
    exchange(5, *second)
    g2r_ref[pl.ds(pi, 1)] = total[None]

    finish(3, "pencil")
    for x in range(0, 4, 2):
        pieces = [recv_ref[3, :, x + i].reshape(R, L) for i in range(2)]
        for i, out in enumerate(stage(zb_ref, pieces)):
            field_ref[x + i, 0:4] = out.astype(BF16).reshape(4, N, L)
    halo = [
        shift(6, field_ref.at[0:2, 0:4], field_ref.at[4:6, 0:4], "slab", -1),
        shift(7, field_ref.at[3:4, 0:4], field_ref.at[6:7, 0:4], "slab", 1),
        shift(8, field_ref.at[0:4, 0:2], field_ref.at[0:4, 4:6], "pencil", -1),
        shift(9, field_ref.at[0:4, 3:4], field_ref.at[0:4, 6:7], "pencil", 1),
    ]
    for copy in halo:
        copy.start()

    arrived(5, *second)
    total = jnp.sum(g2r_ref[...], axis=0)
    g3s_ref[...] = total
    exchange(6, *third)
    g3r_ref[pl.ds(si, 1)] = total[None]

    def gathered(x0, x1, y0, y1):
        depth = (x1 - x0) * (y1 - y0) * N
        return lax.dot_general(
            field_ref[x0:x1, y0:y1].reshape(depth, L), st_ref[x0:x1, y0:y1].reshape(depth, slots),
            (((0,), (0,)), ((), ())), preferred_element_type=F32,
        )

    acc_ref[...] = gathered(0, 4, 0, 4)
    halo[0].wait_recv()
    halo[1].wait_recv()
    corner = [
        shift(10, field_ref.at[4:7, 0:2], field_ref.at[4:7, 4:6], "pencil", -1),
        shift(11, field_ref.at[4:7, 3:4], field_ref.at[4:7, 6:7], "pencil", 1),
    ]
    for copy in corner:
        copy.start()
    acc_ref[...] += gathered(4, 7, 0, 4)
    halo[2].wait_recv()
    halo[3].wait_recv()
    acc_ref[...] += gathered(0, 4, 4, 7)
    corner[0].wait_recv()
    corner[1].wait_recv()
    total = acc_ref[...] + gathered(4, 7, 4, 7)
    pot_ref[...] = total[:C].astype(BF16)
    cg_ref[...] = total[C:].astype(BF16)

    arrived(6, *third)
    for g in range(G):
        grad_ref[g * rows:(g + 1) * rows, :] = g3r_ref[g, 0:rows, 0:C]
    for copy in y_rims + x_rims + halo + corner:
        copy.wait_send()
    for phase, axis in enumerate(["pencil", "slab", "slab", "pencil"]):
        drained(phase, *both_ways(phase, axis))
    drained(4, *first)
    drained(5, *second)
    drained(6, *third)


def per_device(charges, cotangent, base_cell, frac, counts, filter_weights):
    G = lax.axis_size("slab")
    N = 4 * G
    slots = charges.shape[1]
    vmem = pl.BlockSpec(memory_space=pltpu.VMEM)
    smem = pl.BlockSpec(memory_space=pltpu.SMEM)
    scratch = [
        pltpu.VMEM((8, slots), F32),
        pltpu.VMEM((8, slots), F32),
        pltpu.VMEM((N, slots), F32),
        pltpu.VMEM((7, 7, N, slots), BF16),
        pltpu.VMEM((slots, L), BF16),
        pltpu.VMEM((7, 4, N, L), F32),
        pltpu.VMEM((7, 3, N, L), BF16),
        pltpu.VMEM((7, 2, N, L), BF16),
        pltpu.VMEM((7, 1, N, L), BF16),
        pltpu.VMEM((3, 4, N, L), BF16),
        pltpu.VMEM((2, 4, N, L), BF16),
        pltpu.VMEM((1, 4, N, L), BF16),
        pltpu.VMEM((4, G, 4, 16, L), BF16),
        pltpu.VMEM((4, G, 4, 16, L), BF16),
        pltpu.VMEM((16 * N, L), F32),
        pltpu.VMEM((16, N, L), F32),
        pltpu.VMEM((16, N, L), F32),
        pltpu.VMEM((16, N, L), F32),
        pltpu.VMEM((NB, 16 * N), F32),
        pltpu.VMEM((16 * N, L), F32),
        pltpu.VMEM((7, 7, N, L), BF16),
        pltpu.VMEM((L, slots), F32),
        pltpu.VMEM((G, 8, L), F32),
        pltpu.VMEM((G, 8, L), F32),
        pltpu.VMEM((8, L), F32),
        pltpu.VMEM((G, 8, L), F32),
        pltpu.VMEM((8, L), F32),
        pltpu.VMEM((G, 8, L), F32),
        pltpu.SemaphoreType.DMA((12,)),
        pltpu.SemaphoreType.DMA((12,)),
        pltpu.SemaphoreType.DMA((7, G)),
        pltpu.SemaphoreType.DMA((7, G)),
        pltpu.SemaphoreType.DMA((4,)),
    ]
    return pl.pallas_call(
        functools.partial(kernel, G),
        out_shape=(
            jax.ShapeDtypeStruct((C, slots), BF16),
            jax.ShapeDtypeStruct((C, slots), BF16),
            jax.ShapeDtypeStruct((NB, C), F32),
        ),
        in_specs=[smem] + [vmem] * 11,
        out_specs=(vmem, vmem, vmem),
        scratch_shapes=scratch,
        compiler_params=pltpu.CompilerParams(
            collective_id=0, has_side_effects=True, vmem_limit_bytes=48 * 1024 * 1024
        ),
    )(counts, charges, cotangent, base_cell, frac, filter_weights, *tables(G))


def solution(mesh):
    spread = P(None, ("slab", "pencil"))
    return jax.shard_map(
        per_device,
        mesh=mesh,
        in_specs=(spread, spread, spread, spread, P(("slab", "pencil")), P()),
        out_specs=(spread, spread, P()),
        check_vma=False,
    )
```

time: 158 us -> 75.2 us (0.48)
  the two profiles are of different devices: /device:TPU:32 before, /device:TPU:1 now
where the time goes in v2:
time: 75.2 us; the launch traced here: 74.6 us
  Pallas kernels  62.4 us (83%)
  local copies, waits for them, and re-layouts  10.9 us (14%)
  between operations  1.31 us (2%)
    pallas_call x1, Pallas kernels, per_device(): pl.pallas_call(functools.partial(kernel, G), out_shape=(jax.ShapeDtypeStr...  62.4 us
    unnamed x25, local copies, waits for them, and re-layouts  10.9 us

profile of v2, /device:TPU:1, one launch (start us, length us, event | category | flops | bytes accessed | tf_op | source)
XLA Modules:
  0.0 74.6 jit_solution(18429622337201812089)
XLA Ops:
  1.3 0.0 copy-start
  1.3 0.9 %copy-done = bf16[256,512]{1,0:T(8,128)(2,1)S(1)} copy-done((bf16[256,512]{1,0:T(8,128)(2,1)S(1)}, bf16[256,512]{1,0:T(8,128)(2,1)}, u32[]{:S(2)}) %copy-start) | copy-done | bytes 262168
  2.2 0.0 copy-start.1
  2.2 0.9 %copy-done.1 = bf16[256,512]{1,0:T(8,128)(2,1)S(1)} copy-done((bf16[256,512]{1,0:T(8,128)(2,1)S(1)}, bf16[256,512]{1,0:T(8,128)(2,1)}, u32[]{:S(2)}) %copy-start.1) | copy-done | bytes 262168
  3.2 0.0 copy-start.2
  3.2 0.9 %copy-done.2 = bf16[256,512]{1,0:T(8,128)(2,1)S(1)} copy-done((bf16[256,512]{1,0:T(8,128)(2,1)S(1)}, bf16[256,512]{1,0:T(8,128)(2,1)}, u32[]{:S(2)}) %copy-start.2) | copy-done | bytes 262168
  4.1 0.0 copy-start.3
  4.1 0.9 %copy-done.3 = bf16[256,512]{1,0:T(8,128)(2,1)S(1)} copy-done((bf16[256,512]{1,0:T(8,128)(2,1)S(1)}, bf16[256,512]{1,0:T(8,128)(2,1)}, u32[]{:S(2)}) %copy-start.3) | copy-done | bytes 262168
  5.1 0.0 copy-start.4
  5.1 0.8 %copy-done.4 = bf16[64,512]{1,0:T(8,128)(2,1)S(1)} copy-done((bf16[64,512]{1,0:T(8,128)(2,1)S(1)}, bf16[64,512]{1,0:T(8,128)(2,1)}, u32[]{:S(2)}) %copy-start.4) | copy-done | bytes 65560
  5.9 0.0 copy-start.5
  5.9 0.8 %copy-done.5 = bf16[64,512]{1,0:T(8,128)(2,1)S(1)} copy-done((bf16[64,512]{1,0:T(8,128)(2,1)S(1)}, bf16[64,512]{1,0:T(8,128)(2,1)}, u32[]{:S(2)}) %copy-start.5) | copy-done | bytes 65560
  6.8 0.0 copy-start.6
  6.8 0.8 %copy-done.6 = bf16[128,128]{1,0:T(8,128)(2,1)S(1)} copy-done((bf16[128,128]{1,0:T(8,128)(2,1)S(1)}, bf16[128,128]{1,0:T(8,128)(2,1)}, u32[]{:S(2)}) %copy-start.6) | copy-done | bytes 32792
  7.5 0.0 copy-start.7
  7.5 0.7 copy-done.7
  8.2 0.0 copy-start.8
  8.2 0.7 copy-done.8
  9.0 0.0 copy-start.9
  9.0 0.7 copy-done.9
  9.7 0.0 copy-start.10
  9.7 0.7 copy-done.10
  10.4 62.4 %shard_map.148 = (bf16[64,512]{1,0:T(8,128)(2,1)S(1)}, bf16[64,512]{1,0:T(8,128)(2,1)S(1)}, f32[32,64]{1,0:T(8,128)S(1)}) custom-call(s32[1]{0:T(128)S(6)} %copy.19.count_ref, bf16[64,512]{1,0:T(8,128)(2,1)S(1)} %copy-done.4, bf16[64,512]{1,0:T(8,128)(2,1)S(1)} %copy-done.5, s32[3,512]{1,0:T(4,128)S(1)} %copy-done.9, f32[3,512]{1,0:T(4,128)S(1)} %copy-done.10, ...), custom_call_target="tpu_custom_call" | custom-call | tf_op jit(solution)/shard_map/pallas_call | solution.py:405
  72.8 0.6 copy.20
  73.4 0.6 copy.21
  74.0 0.6 copy.22
Async XLA Ops:
  1.3 1.0 %copy-start = (bf16[256,512]{1,0:T(8,128)(2,1)S(1)}, bf16[256,512]{1,0:T(8,128)(2,1)}, u32[]{:S(2)}) copy-start(bf16[256,512]{1,0:T(8,128)(2,1)} %constant.20.clone.zb_ref) | copy-start | bytes 786436
  2.2 0.9 %copy-start.1 = (bf16[256,512]{1,0:T(8,128)(2,1)S(1)}, bf16[256,512]{1,0:T(8,128)(2,1)}, u32[]{:S(2)}) copy-start(bf16[256,512]{1,0:T(8,128)(2,1)} %constant.19.clone.yb_ref) | copy-start | bytes 786436
  3.2 0.9 %copy-start.2 = (bf16[256,512]{1,0:T(8,128)(2,1)S(1)}, bf16[256,512]{1,0:T(8,128)(2,1)}, u32[]{:S(2)}) copy-start(bf16[256,512]{1,0:T(8,128)(2,1)} %constant.15.clone.ya_ref) | copy-start | bytes 786436
  4.1 0.9 %copy-start.3 = (bf16[256,512]{1,0:T(8,128)(2,1)S(1)}, bf16[256,512]{1,0:T(8,128)(2,1)}, u32[]{:S(2)}) copy-start(bf16[256,512]{1,0:T(8,128)(2,1)} %constant.14.clone.za_ref) | copy-start | bytes 786436
  5.1 0.8 %copy-start.4 = (bf16[64,512]{1,0:T(8,128)(2,1)S(1)}, bf16[64,512]{1,0:T(8,128)(2,1)}, u32[]{:S(2)}) copy-start(bf16[64,512]{1,0:T(8,128)(2,1)} %charges_ref.1) | copy-start | bytes 196612
  5.9 0.8 %copy-start.5 = (bf16[64,512]{1,0:T(8,128)(2,1)S(1)}, bf16[64,512]{1,0:T(8,128)(2,1)}, u32[]{:S(2)}) copy-start(bf16[64,512]{1,0:T(8,128)(2,1)} %cot_ref.1) | copy-start | bytes 196612
  6.8 0.8 %copy-start.6 = (bf16[128,128]{1,0:T(8,128)(2,1)S(1)}, bf16[128,128]{1,0:T(8,128)(2,1)}, u32[]{:S(2)}) copy-start(bf16[128,128]{1,0:T(8,128)(2,1)} %constant.22.xa_ref) | copy-start | bytes 98308
  7.5 0.7 copy-start.7
  8.2 0.7 copy-start.8
  9.0 0.7 copy-start.9
  9.7 0.7 copy-start.10

commit v3 on v1

v3 whole, which is shorter than its diff:
```python
import functools

import jax
import jax.numpy as jnp
import numpy as np
from jax import lax
from jax.experimental import pallas as pl
from jax.experimental.pallas import tpu as pltpu
from jax.sharding import PartitionSpec as P

C = 64
L = 2 * C
NB = 32
ENV_SCALE = 40.0
ENV_WIDTH = 16.0
MESH = pl.DeviceIdType.MESH
F32 = jnp.float32
BF16 = jnp.bfloat16


def wave_order(groups):
    count = 4 * groups
    rows = []
    for g in range(groups):
        rows += [2 * g, 2 * g + 1, count - 2 * g if g else count // 2, count - 1 - 2 * g]
    return np.array(rows)


def tables(groups):
    count = 4 * groups
    waves = wave_order(groups)
    eye = np.eye(4)

    def parts(rows, cells, inverse):
        angles = (rows[:, None] * cells[None, :] % count) * (2.0 * np.pi / count)
        cosines, sines = np.cos(angles), np.sin(angles)
        return (cosines.T / count, -sines.T / count) if inverse else (cosines, sines)

    def joined(pair, pattern=None, inner=eye):
        size = 4 * count
        if pattern is not None:
            split = [t.reshape(groups, 4, groups, 4) for t in pair]
            pair = [np.einsum(pattern, t, inner).reshape(size, size) for t in split]
        return np.concatenate(pair, axis=1)

    every = np.arange(count)
    wide = (4 * np.arange(groups)[:, None] + np.arange(7)[None, :]).reshape(-1)
    ahead, back = parts(waves, every, False), parts(waves, every, True)
    mirror = parts((-waves) % count, every, False)
    y_ahead = joined(ahead, "glhm,ab->glahmb")
    across = [np.eye(4)[[(a + 2) % 4 for a in range(4)]], np.eye(4)[[(4 - a) % 4 for a in range(4)]]]
    made = [
        joined(ahead, "glhm,yv->gylvhm"),
        joined(parts(waves, wide, False)),
        np.stack([np.concatenate([y_ahead, joined(mirror, "glhm,ab->glahmb", t)]) for t in across]),
        joined(back, "glhm,ab->glahmb"),
        joined(parts(waves, wide, True)),
        joined(back, "glhm,yv->yglhvm"),
    ]
    return [jnp.asarray(t, BF16) for t in made]


def spline_weights(frac):
    remain = 1.0 - frac
    square = frac * frac
    cubed = square * frac
    return [
        remain * remain * remain / 6.0,
        (3.0 * cubed - 6.0 * square + 4.0) / 6.0,
        (-3.0 * cubed + 3.0 * square + 3.0 * frac + 1.0) / 6.0,
        cubed / 6.0,
    ]


def placed(gap, weights):
    out = jnp.zeros(gap.shape, F32)
    for j in range(4):
        out = jnp.where(gap == j, weights[j], out)
    return out


def squared_wave(group, inner, count):
    wave = jnp.where(inner < 2, 2 * group + inner, count - 2 * group - inner + 2)
    wave = jnp.where((inner == 2) & (group == 0), count // 2, wave)
    wave = jnp.where(wave < count // 2, wave, wave - count)
    return wave * wave


def kernel(
    groups, count_ref, charges_hbm, cot_hbm, base_hbm, frac_hbm, weights_hbm,
    za_hbm, xa_hbm, ya_hbm, yb_hbm, xb_hbm, zb_hbm,
    pot_ref, cg_ref, grad_ref,
    base_ref, frac_ref, both_ref, weights_ref, za_ref, xa_ref, ya_ref, yb_ref, xb_ref, zb_ref, load_sem,
    par_ref, near_par_ref, near_ref, wx_ref, wy_ref, wz_ref, st_ref, sn_ref, vals_ref, den_ref,
    s0_ref, r0_ref, s1_ref, r1_ref, s2_ref, r2_ref, s3_ref, r3_ref,
    wide_ref, line_ref, spec_ref, mirror_ref, prof_ref, shell_ref, corr_ref, field_ref, acc_ref, part_ref, back_ref,
    g1s_ref, g1r_ref, g2s_ref, g2r_ref, g3s_ref, g3r_ref,
    hs, hr, es, er, local_sem,
):
    G = groups
    N = 4 * G
    R = 4 * N
    si = lax.axis_index("slab")
    pi = lax.axis_index("pencil")
    where_is = {"slab": si, "pencil": pi}
    slots = charges_hbm.shape[1]

    barrier = pltpu.get_barrier_semaphore()

    def greet(d, carry):
        pl.semaphore_signal(barrier, inc=1, device_id={"pencil": lax.rem(pi + d, G)}, device_id_type=MESH)
        pl.semaphore_signal(barrier, inc=1, device_id={"slab": lax.rem(si + d, G)}, device_id_type=MESH)
        return carry

    lax.fori_loop(1, G, greet, 0)

    pairs = [
        (base_hbm, base_ref), (frac_hbm, frac_ref), (charges_hbm, both_ref.at[0:C]), (cot_hbm, both_ref.at[C:L]),
        (za_hbm, za_ref), (weights_hbm, weights_ref), (xa_hbm, xa_ref), (ya_hbm, ya_ref),
        (yb_hbm, yb_ref), (xb_hbm, xb_ref), (zb_hbm, zb_ref),
    ]
    owed = {}
    for i, (src, dst) in enumerate(pairs):
        load = pltpu.make_async_copy(src, dst, load_sem.at[i])
        load.start()
        owed["load", i] = load.wait

    def settle(*keys):
        for key in keys:
            owed.pop(key)()

    def shift(i, src, dst, step):
        copy = pltpu.make_async_remote_copy(
            src_ref=src, dst_ref=dst, send_sem=hs.at[i], recv_sem=hr.at[i],
            device_id={"pencil": lax.rem(pi + step + G, G)}, device_id_type=MESH,
        )
        copy.start()
        owed["shift", i] = copy.wait_recv
        owed["sent", i] = copy.wait_send

    def exchange(phase, src_of, dst, axis):
        me = where_is[axis]

        def hop(d, landed):
            peer = lax.rem(me + d, G)
            return pltpu.make_async_remote_copy(
                src_ref=src_of(peer), dst_ref=dst.at[landed], send_sem=es.at[phase, d], recv_sem=er.at[phase, d],
                device_id={axis: peer}, device_id_type=MESH,
            )

        def start(d, carry):
            hop(d, me).start()
            return carry

        def arrive(d, carry):
            hop(d, lax.rem(me + G - d, G)).wait_recv()
            return carry

        def drain(d, carry):
            hop(d, me).wait_send()
            return carry

        lax.fori_loop(1, G, start, 0)
        owed["exchange", phase] = lambda: lax.fori_loop(1, G, arrive, 0)
        owed["gone", phase] = lambda: lax.fori_loop(1, G, drain, 0)

    def begin(phase, src, dst, axis):
        me = where_is[axis]
        exchange(phase, lambda peer: src.at[peer], dst, axis)
        own = pltpu.make_async_copy(src.at[me], dst.at[me], local_sem.at[phase])
        own.start()
        owed["own", phase] = own.wait

    def finish(phase):
        settle(("exchange", phase), ("own", phase))

    lane = lax.broadcasted_iota(jnp.int32, (1, L), 1)
    sign = jnp.where(lane < C, 1.0, -1.0).astype(F32)

    def stage(table, pieces):
        columns = []
        for piece in pieces:
            wide = piece.astype(F32)
            turned = (pltpu.roll(wide, C, 1) * sign).astype(BF16)
            columns.append(jnp.concatenate([piece.astype(BF16), turned], axis=0))
        out = jnp.dot(table, jnp.concatenate(columns, axis=1), preferred_element_type=F32)
        return [out[:, i * L:(i + 1) * L] for i in range(len(pieces))]

    settle(("load", 0), ("load", 1))
    live = lax.broadcasted_iota(jnp.int32, (1, slots), 1) < count_ref[0]
    par_ref[0:3, :] = frac_ref[...]
    par_ref[3:6, :] = base_ref[...].astype(F32)
    par_ref[6:7, :] = live.astype(F32)
    par_ref[7:8, :] = jnp.zeros((1, slots), F32)
    settle(("load", 2), ("load", 3))
    pl.semaphore_wait(barrier, 2 * (G - 1))
    shift(0, par_ref, near_par_ref, 1)
    shift(1, both_ref, near_ref, 1)

    def weigh(par, block, first_row):
        row = lax.broadcasted_iota(jnp.int32, (8, slots), 0).astype(F32)
        wx = placed(row - (par[3:4, :] - (4 * si).astype(F32)), spline_weights(par[0:1, :]))
        wx_ref[...] = wx * par[6:7, :]
        wy_ref[...] = placed(row + first_row - (par[4:5, :] - (4 * block).astype(F32)), spline_weights(par[1:2, :]))
        gap = lax.broadcasted_iota(jnp.int32, (N, slots), 0).astype(F32) - par[5:6, :]
        wz_ref[...] = placed(jnp.where(gap < 0, gap + N, gap), spline_weights(par[2:3, :]))

    def spread(stencil_ref, x, rows):
        along_x = wx_ref[pl.ds(x, 1), :]
        for y in range(rows):
            stencil_ref[x, y] = (wz_ref[...] * (along_x * wy_ref[y:y + 1, :])).astype(BF16)
        left = stencil_ref[x].reshape(rows * N, slots)
        return jnp.dot(left, vals_ref[...], preferred_element_type=F32)

    def own_plane(x, carry):
        den_ref[x] = spread(st_ref, x, 4)
        return carry

    def near_plane(x, carry):
        den_ref[x, 0:3 * N] += spread(sn_ref, x, 3)
        return carry

    weigh(par_ref, pi, 0.0)
    vals_ref[...] = both_ref[...].T
    lax.fori_loop(0, 7, own_plane, 0)
    settle(("load", 4), ("shift", 0), ("shift", 1))
    weigh(near_par_ref, lax.rem(pi + G - 1, G), 4.0)
    vals_ref[...] = near_ref[...].T
    lax.fori_loop(0, 7, near_plane, 0)
    for x in range(0, 7, 2):
        pieces = [den_ref[i] for i in range(x, min(x + 2, 7))]
        for i, out in enumerate(stage(za_ref[...], pieces)):
            s0_ref[:, x + i] = out.astype(BF16).reshape(G, 16, L)
    begin(0, s0_ref, r0_ref, "slab")

    settle(*[("load", i) for i in range(5, 11)])
    at = lax.broadcasted_iota(jnp.int32, (NB, 16 * N), 1)
    along = at // 4 % N
    kappa_sq = (
        squared_wave(pi, at // R, N) + squared_wave(along // 4, along % 4, N) + squared_wave(si, at % 4, N)
    ).astype(F32)
    spacing = N / (2.0 * NB)
    centers = (lax.broadcasted_iota(jnp.int32, (NB, 16 * N), 0).astype(F32) + 0.5) * spacing
    reach = (jnp.sqrt(kappa_sq) - centers) / spacing
    shell_ref[...] = ENV_SCALE * ENV_WIDTH / (ENV_WIDTH + kappa_sq) * jnp.exp(-(reach * reach))
    doubled = jnp.concatenate([weights_ref[...], weights_ref[...]], axis=1)
    prof_ref[...] = lax.dot_general(
        shell_ref[...], doubled, (((0,), (0,)), ((), ())),
        precision=lax.Precision.HIGHEST, preferred_element_type=F32,
    ).reshape(4, R, L)

    finish(0)
    wide_ref[...] = r0_ref[...].reshape(7 * 16 * G, L).astype(F32)
    for b in range(0, 16, 2):
        outs = stage(xa_ref[...], [wide_ref[pl.ds(b + i, 7 * G, stride=16), :] for i in range(2)])
        for i in range(2):
            line_ref[pl.ds(b + i, N, stride=16), :] = outs[i]
    s1_ref[...] = line_ref[...].astype(BF16).reshape(G, 4, 16, L)
    begin(1, s1_ref, r1_ref, "pencil")
    finish(1)

    flip = jnp.where(si == 0, 1, 0)
    for x in range(0, 4, 2):
        outs = stage(ya_ref[flip], [r1_ref[:, x + i].reshape(R, L) for i in range(2)])
        for i in range(2):
            spec_ref[x + i] = outs[i][:R]
            mirror_ref[x + i] = outs[i][R:]
        outs = stage(yb_ref[...], [spec_ref[x + i] * prof_ref[x + i] for i in range(2)])
        for i in range(2):
            s2_ref[:, x + i] = outs[i].astype(BF16).reshape(G, 16, L)
    begin(2, s2_ref, r2_ref, "pencil")

    for x in range(4):
        opposite = jnp.where(pi == 0, (4 - x) % 4, (x + 2) % 4)
        corr_ref[pl.ds(x * R, R), :] = spec_ref[x] * pltpu.roll(mirror_ref[opposite], C, 1)
    partial = jnp.dot(
        shell_ref[...], corr_ref[...], precision=lax.Precision.HIGHEST, preferred_element_type=F32
    )
    partial = (partial + pltpu.roll(partial, C, 1)) * (0.5 / (N * N * N))
    rows = NB // G
    g1s_ref[...] = jnp.zeros_like(g1s_ref)
    for g in range(G):
        g1s_ref[g, 0:rows, :] = partial[g * rows:(g + 1) * rows]
    exchange(4, lambda peer: g1s_ref.at[peer], g1r_ref, "pencil")
    g1r_ref[pl.ds(pi, 1)] = g1s_ref[pl.ds(pi, 1)]

    finish(2)
    line_ref[...] = r2_ref[...].reshape(16 * N, L).astype(F32)
    for b in range(0, 16, 2):
        outs = stage(xb_ref[...], [line_ref[pl.ds(b + i, N, stride=16), :] for i in range(2)])
        for i in range(2):
            wide_ref[pl.ds(b + i, 7 * G, stride=16), :] = outs[i]
    s3_ref[...] = wide_ref[...].astype(BF16).reshape(G, 7, 16, L)
    begin(3, s3_ref, r3_ref, "slab")

    settle(("exchange", 4))
    total = jnp.sum(g1r_ref[...], axis=0)
    g2s_ref[...] = total
    exchange(5, lambda peer: g2s_ref, g2r_ref, "slab")
    g2r_ref[pl.ds(si, 1)] = total[None]

    finish(3)
    for x in range(0, 7, 2):
        pieces = [r3_ref[:, i].reshape(R, L) for i in range(x, min(x + 2, 7))]
        for i, out in enumerate(stage(zb_ref[...], pieces)):
            field_ref[x + i] = out.astype(BF16)

    def gathered(stencil_ref, rows):
        depth = 7 * rows * N
        return lax.dot_general(
            field_ref[:, 0:rows * N].reshape(depth, L), stencil_ref[...].reshape(depth, slots),
            (((0,), (0,)), ((), ())), preferred_element_type=F32,
        )

    part_ref[...] = gathered(sn_ref, 3).astype(BF16)
    shift(2, part_ref, back_ref, -1)

    settle(("exchange", 5))
    total = jnp.sum(g2r_ref[...], axis=0)
    g3s_ref[...] = total
    exchange(6, lambda peer: g3s_ref, g3r_ref, "pencil")
    g3r_ref[pl.ds(pi, 1)] = total[None]

    acc_ref[...] = gathered(st_ref, 4)
    settle(("shift", 2))
    pot_ref[...] = (acc_ref[0:C] + back_ref[0:C].astype(F32)).astype(BF16)
    cg_ref[...] = (acc_ref[C:L] + back_ref[C:L].astype(F32)).astype(BF16)

    settle(("exchange", 6))
    for g in range(G):
        grad_ref[g * rows:(g + 1) * rows, :] = g3r_ref[g, 0:rows, 0:C]
    for wait in owed.values():
        wait()


def per_device(charges, cotangent, base_cell, frac, counts, filter_weights):
    G = lax.axis_size("slab")
    N = 4 * G
    slots = charges.shape[1]
    dft = tables(G)
    vmem = pl.BlockSpec(memory_space=pltpu.VMEM)
    smem = pl.BlockSpec(memory_space=pltpu.SMEM)
    hbm = pl.BlockSpec(memory_space=pltpu.HBM)
    wide = pltpu.VMEM((G, 7, 16, L), BF16)
    slim = pltpu.VMEM((G, 4, 16, L), BF16)
    tiles = pltpu.VMEM((G, 8, L), F32)
    tile = pltpu.VMEM((8, L), F32)
    scratch = [
        pltpu.VMEM((3, slots), jnp.int32),
        pltpu.VMEM((3, slots), F32),
        pltpu.VMEM((L, slots), BF16),
        pltpu.VMEM((NB, C), F32),
        *[pltpu.VMEM(t.shape, BF16) for t in dft],
        pltpu.SemaphoreType.DMA((11,)),
        pltpu.VMEM((8, slots), F32),
        pltpu.VMEM((8, slots), F32),
        pltpu.VMEM((L, slots), BF16),
        pltpu.VMEM((8, slots), F32),
        pltpu.VMEM((8, slots), F32),
        pltpu.VMEM((N, slots), F32),
        pltpu.VMEM((7, 4, N, slots), BF16),
        pltpu.VMEM((7, 3, N, slots), BF16),
        pltpu.VMEM((slots, L), BF16),
        pltpu.VMEM((7, 4 * N, L), F32),
        wide, wide, slim, slim, slim, slim, wide, wide,
        pltpu.VMEM((7 * 16 * G, L), F32),
        pltpu.VMEM((16 * N, L), F32),
        pltpu.VMEM((4, 4 * N, L), F32),
        pltpu.VMEM((4, 4 * N, L), F32),
        pltpu.VMEM((4, 4 * N, L), F32),
        pltpu.VMEM((NB, 16 * N), F32),
        pltpu.VMEM((16 * N, L), F32),
        pltpu.VMEM((7, 4 * N, L), BF16),
        pltpu.VMEM((L, slots), F32),
        pltpu.VMEM((L, slots), BF16),
        pltpu.VMEM((L, slots), BF16),
        tiles, tiles, tile, tiles, tile, tiles,
        pltpu.SemaphoreType.DMA((3,)),
        pltpu.SemaphoreType.DMA((3,)),
        pltpu.SemaphoreType.DMA((7, G)),
        pltpu.SemaphoreType.DMA((7, G)),
        pltpu.SemaphoreType.DMA((4,)),
    ]
    return pl.pallas_call(
        functools.partial(kernel, G),
        out_shape=(
            jax.ShapeDtypeStruct((C, slots), BF16),
            jax.ShapeDtypeStruct((C, slots), BF16),
            jax.ShapeDtypeStruct((NB, C), F32),
        ),
        in_specs=[smem] + [hbm] * 11,
        out_specs=(vmem, vmem, vmem),
        scratch_shapes=scratch,
        compiler_params=pltpu.CompilerParams(
            collective_id=0, has_side_effects=True, vmem_limit_bytes=67043328
        ),
    )(counts, charges, cotangent, base_cell, frac, filter_weights, *dft)


def solution(mesh):
    spread = P(None, ("slab", "pencil"))
    return jax.shard_map(
        per_device,
        mesh=mesh,
        in_specs=(spread, spread, spread, spread, P(("slab", "pencil")), P()),
        out_specs=(spread, spread, P()),
        check_vma=False,
    )
```

time: 158 us -> 66.7 us (0.42)
  the two profiles are of different devices: /device:TPU:32 before, /device:TPU:1 now
where the time goes in v3:
time: 66.7 us; the launch traced here: 66.5 us
  Pallas kernels  62.3 us (93%)
  local copies, waits for them, and re-layouts  2.83 us (4%)
  between operations  1.3 us (2%)
    pallas_call x1, Pallas kernels, per_device(): pl.pallas_call(functools.partial(kernel, G), out_shape=(jax.ShapeDtypeStr...  62.3 us
    unnamed x7, local copies, waits for them, and re-layouts  2.83 us

profile of v3, /device:TPU:1, one launch (start us, length us, event | category | flops | bytes accessed | tf_op | source)
XLA Modules:
  0.0 66.5 jit_solution(7835790434466675)
XLA Ops:
  1.3 62.3 %shard_map.139 = (bf16[64,512]{1,0:T(8,128)(2,1)}, bf16[64,512]{1,0:T(8,128)(2,1)}, f32[32,64]{1,0:T(8,128)}) custom-call(s32[1]{0:T(128)S(6)} %copy.18.count_ref, bf16[64,512]{1,0:T(8,128)(2,1)} %charges_hbm.1, bf16[64,512]{1,0:T(8,128)(2,1)} %cot_hbm.1, s32[3,512]{1,0:T(4,128)} %base_hbm.1, f32[3,512]{1,0:T(4,128)} %frac_hbm.1, f32[32,64]{1,0:T(8,128)} %weights_hbm.1, ...), custom_call_target="tpu_custom_call" | custom-call | tf_op jit(solution)/shard_map/pallas_call | solution.py:384
  63.6 0.0 copy-start
  63.6 1.5 %copy.19 = bf16[64,512]{1,0:T(8,128)(2,1)} copy(bf16[64,512]{1,0:T(8,128)(2,1)} %get-tuple-element.6) | data formatting | bytes 131072
  65.1 0.0 copy-done
  65.1 0.0 copy-start.1
  65.2 0.6 copy.20
  65.8 0.1 copy-done.1
  65.9 0.6 copy.21
Async XLA Ops:
  63.6 1.5 %copy-start = (bf16[64,512]{1,0:T(8,128)(2,1)S(1)}, bf16[64,512]{1,0:T(8,128)(2,1)}, u32[]{:S(2)}) copy-start(bf16[64,512]{1,0:T(8,128)(2,1)} %get-tuple-element.7) | copy-start | bytes 196612
  65.1 0.7 %copy-start.1 = (f32[32,64]{1,0:T(8,128)S(1)}, f32[32,64]{1,0:T(8,128)}, u32[]{:S(2)}) copy-start(f32[32,64]{1,0:T(8,128)} %get-tuple-element.8) | copy-start | bytes 24580

commit v4 on v3

--- a/solution.py
+++ b/solution.py
@@ -84,6 +84,14 @@
     wave = jnp.where((inner == 2) & (group == 0), count // 2, wave)
     wave = jnp.where(wave < count // 2, wave, wave - count)
     return wave * wave
+
+
+def hop_order(major, minor):
+    def far(step, size):
+        return min(step, size - step)
+
+    steps = [(a, b) for a in range(major) for b in range(minor) if a or b]
+    return sorted(steps, key=lambda s: (-far(s[0], major) - far(s[1], minor), abs(far(s[0], major) - far(s[1], minor)), s))
 
 
 def kernel(
@@ -141,28 +149,16 @@
     def exchange(phase, src_of, dst, axis):
         me = where_is[axis]
 
-        def hop(d, landed):
-            peer = lax.rem(me + d, G)
-            return pltpu.make_async_remote_copy(
-                src_ref=src_of(peer), dst_ref=dst.at[landed], send_sem=es.at[phase, d], recv_sem=er.at[phase, d],
+        inner = 4 if axis == "slab" and G == 16 else 2
+        for major, minor in hop_order(G // inner, inner):
+            peer = lax.rem(lax.div(me, inner) + major, G // inner) * inner + lax.rem(lax.rem(me, inner) + minor, inner)
+            pltpu.make_async_remote_copy(
+                src_ref=src_of(peer), dst_ref=dst.at[me], send_sem=es.at[phase], recv_sem=er.at[phase],
                 device_id={axis: peer}, device_id_type=MESH,
-            )
-
-        def start(d, carry):
-            hop(d, me).start()
-            return carry
-
-        def arrive(d, carry):
-            hop(d, lax.rem(me + G - d, G)).wait_recv()
-            return carry
-
-        def drain(d, carry):
-            hop(d, me).wait_send()
-            return carry
-
-        lax.fori_loop(1, G, start, 0)
-        owed["exchange", phase] = lambda: lax.fori_loop(1, G, arrive, 0)
-        owed["gone", phase] = lambda: lax.fori_loop(1, G, drain, 0)
+            ).start()
+        others = dst.at[0:G - 1]
+        owed["exchange", phase] = pltpu.make_async_copy(others, others, er.at[phase]).wait
+        owed["gone", phase] = pltpu.make_async_copy(others, others, es.at[phase]).wait
 
     def begin(phase, src, dst, axis):
         me = where_is[axis]
@@ -377,8 +373,8 @@
         tiles, tiles, tile, tiles, tile, tiles,
         pltpu.SemaphoreType.DMA((3,)),
         pltpu.SemaphoreType.DMA((3,)),
-        pltpu.SemaphoreType.DMA((7, G)),
-        pltpu.SemaphoreType.DMA((7, G)),
+        pltpu.SemaphoreType.DMA((7,)),
+        pltpu.SemaphoreType.DMA((7,)),
         pltpu.SemaphoreType.DMA((4,)),
     ]
     return pl.pallas_call(

time: 66.7 us -> 57.7 us (0.87)
  Pallas kernels: 62.3 us -> 53.3 us
    pallas_call x1, Pallas kernels: 62.3 us -> 53.3 us  [per_device(): pl.pallas_call(functools.partial(kernel, G), out_shape=(jax.ShapeDtypeStr...]
where the time goes in v4:
time: 57.7 us; the launch traced here: 57.4 us
  Pallas kernels  53.3 us (92%)
  local copies, waits for them, and re-layouts  2.83 us (5%)
  between operations  1.3 us (2%)
    pallas_call x1, Pallas kernels, per_device(): pl.pallas_call(functools.partial(kernel, G), out_shape=(jax.ShapeDtypeStr...  53.3 us
    unnamed x7, local copies, waits for them, and re-layouts  2.83 us

profile of v4, /device:TPU:1, one launch (start us, length us, event | category | flops | bytes accessed | tf_op | source)
XLA Modules:
  0.0 57.4 jit_solution(12292804513992078873)
XLA Ops:
  1.3 53.3 %shard_map.139 = (bf16[64,512]{1,0:T(8,128)(2,1)}, bf16[64,512]{1,0:T(8,128)(2,1)}, f32[32,64]{1,0:T(8,128)}) custom-call(s32[1]{0:T(128)S(6)} %copy.18.count_ref, bf16[64,512]{1,0:T(8,128)(2,1)} %charges_hbm.1, bf16[64,512]{1,0:T(8,128)(2,1)} %cot_hbm.1, s32[3,512]{1,0:T(4,128)} %base_hbm.1, f32[3,512]{1,0:T(4,128)} %frac_hbm.1, f32[32,64]{1,0:T(8,128)} %weights_hbm.1, ...), custom_call_target="tpu_custom_call" | custom-call | tf_op jit(solution)/shard_map/pallas_call | solution.py:380
  54.6 0.0 copy-start
  54.6 1.5 %copy.19 = bf16[64,512]{1,0:T(8,128)(2,1)} copy(bf16[64,512]{1,0:T(8,128)(2,1)} %get-tuple-element.6) | data formatting | bytes 131072
  56.1 0.0 copy-done
  56.1 0.0 copy-start.1
  56.1 0.6 %copy.20 = bf16[64,512]{1,0:T(8,128)(2,1)} copy(bf16[64,512]{1,0:T(8,128)(2,1)S(1)} %copy-done) | data formatting | bytes 131072
  56.8 0.1 copy-done.1
  56.8 0.6 %copy.21 = f32[32,64]{1,0:T(8,128)} copy(f32[32,64]{1,0:T(8,128)S(1)} %copy-done.1) | data formatting | bytes 16384
Async XLA Ops:
  54.6 1.5 %copy-start = (bf16[64,512]{1,0:T(8,128)(2,1)S(1)}, bf16[64,512]{1,0:T(8,128)(2,1)}, u32[]{:S(2)}) copy-start(bf16[64,512]{1,0:T(8,128)(2,1)} %get-tuple-element.7) | copy-start | bytes 196612
  56.1 0.7 %copy-start.1 = (f32[32,64]{1,0:T(8,128)S(1)}, f32[32,64]{1,0:T(8,128)}, u32[]{:S(2)}) copy-start(f32[32,64]{1,0:T(8,128)} %get-tuple-element.8) | copy-start | bytes 24580

commit v5 on v4

--- a/solution.py
+++ b/solution.py
@@ -49,13 +49,16 @@
     mirror = parts((-waves) % count, every, False)
     y_ahead = joined(ahead, "glhm,ab->glahmb")
     across = [np.eye(4)[[(a + 2) % 4 for a in range(4)]], np.eye(4)[[(4 - a) % 4 for a in range(4)]]]
+    halves = np.arange(4 * count).reshape(groups, 2, 2, 4).transpose(1, 0, 2, 3).reshape(-1)
+    paired = np.concatenate([halves, halves + 4 * count])
     made = [
-        joined(ahead, "glhm,yv->gylvhm"),
+        joined(ahead, "glhm,yv->gylvhm")[halves],
         joined(parts(waves, wide, False)),
-        np.stack([np.concatenate([y_ahead, joined(mirror, "glhm,ab->glahmb", t)]) for t in across]),
-        joined(back, "glhm,ab->glahmb"),
+        y_ahead[:, paired],
+        np.stack([joined(mirror, "glhm,ab->glahmb", t)[:, paired] for t in across]),
+        joined(back, "glhm,ab->glahmb")[halves],
         joined(parts(waves, wide, True)),
-        joined(back, "glhm,yv->yglhvm"),
+        joined(back, "glhm,yv->yglhvm")[:, paired],
     ]
     return [jnp.asarray(t, BF16) for t in made]
 
@@ -96,10 +99,10 @@
 
 def kernel(
     groups, count_ref, charges_hbm, cot_hbm, base_hbm, frac_hbm, weights_hbm,
-    za_hbm, xa_hbm, ya_hbm, yb_hbm, xb_hbm, zb_hbm,
+    za_hbm, xa_hbm, ya_hbm, ym_hbm, yb_hbm, xb_hbm, zb_hbm,
     pot_ref, cg_ref, grad_ref,
-    base_ref, frac_ref, both_ref, weights_ref, za_ref, xa_ref, ya_ref, yb_ref, xb_ref, zb_ref, load_sem,
-    par_ref, near_par_ref, near_ref, wx_ref, wy_ref, wz_ref, st_ref, sn_ref, vals_ref, den_ref,
+    base_ref, frac_ref, both_ref, weights_ref, za_ref, xa_ref, ya_ref, ym_ref, yb_ref, xb_ref, zb_ref, load_sem,
+    live_ref, near_live_ref, near_frac_ref, near_base_ref, near_ref, wx_ref, wy_ref, wz_ref, st_ref, sn_ref, vals_ref, den_ref,
     s0_ref, r0_ref, s1_ref, r1_ref, s2_ref, r2_ref, s3_ref, r3_ref,
     wide_ref, line_ref, spec_ref, mirror_ref, prof_ref, shell_ref, corr_ref, field_ref, acc_ref, part_ref, back_ref,
     g1s_ref, g1r_ref, g2s_ref, g2r_ref, g3s_ref, g3r_ref,
@@ -125,6 +128,7 @@
     pairs = [
         (base_hbm, base_ref), (frac_hbm, frac_ref), (charges_hbm, both_ref.at[0:C]), (cot_hbm, both_ref.at[C:L]),
         (za_hbm, za_ref), (weights_hbm, weights_ref), (xa_hbm, xa_ref), (ya_hbm, ya_ref),
+        (ym_hbm, ym_ref),
         (yb_hbm, yb_ref), (xb_hbm, xb_ref), (zb_hbm, zb_ref),
     ]
     owed = {}
@@ -182,24 +186,21 @@
         out = jnp.dot(table, jnp.concatenate(columns, axis=1), preferred_element_type=F32)
         return [out[:, i * L:(i + 1) * L] for i in range(len(pieces))]
 
-    settle(("load", 0), ("load", 1))
-    live = lax.broadcasted_iota(jnp.int32, (1, slots), 1) < count_ref[0]
-    par_ref[0:3, :] = frac_ref[...]
-    par_ref[3:6, :] = base_ref[...].astype(F32)
-    par_ref[6:7, :] = live.astype(F32)
-    par_ref[7:8, :] = jnp.zeros((1, slots), F32)
-    settle(("load", 2), ("load", 3))
+    live = lax.broadcasted_iota(jnp.int32, (8, slots), 1) < count_ref[0]
+    live_ref[...] = live.astype(F32)
     pl.semaphore_wait(barrier, 2 * (G - 1))
-    shift(0, par_ref, near_par_ref, 1)
-    shift(1, both_ref, near_ref, 1)
-
-    def weigh(par, block, first_row):
-        row = lax.broadcasted_iota(jnp.int32, (8, slots), 0).astype(F32)
-        wx = placed(row - (par[3:4, :] - (4 * si).astype(F32)), spline_weights(par[0:1, :]))
-        wx_ref[...] = wx * par[6:7, :]
-        wy_ref[...] = placed(row + first_row - (par[4:5, :] - (4 * block).astype(F32)), spline_weights(par[1:2, :]))
-        gap = lax.broadcasted_iota(jnp.int32, (N, slots), 0).astype(F32) - par[5:6, :]
-        wz_ref[...] = placed(jnp.where(gap < 0, gap + N, gap), spline_weights(par[2:3, :]))
+    shift(0, charges_hbm, near_ref.at[0:C], 1)
+    shift(1, cot_hbm, near_ref.at[C:L], 1)
+    shift(2, frac_hbm, near_frac_ref, 1)
+    shift(3, base_hbm, near_base_ref, 1)
+    shift(4, live_ref, near_live_ref, 1)
+
+    def weigh(frac, base, alive, block, first_row):
+        row = lax.broadcasted_iota(jnp.int32, (8, slots), 0)
+        wx_ref[...] = placed(row - (base[0:1, :] - 4 * si), spline_weights(frac[0:1, :])) * alive[...]
+        wy_ref[...] = placed(row + first_row - (base[1:2, :] - 4 * block), spline_weights(frac[1:2, :]))
+        gap = lax.broadcasted_iota(jnp.int32, (N, slots), 0) - base[2:3, :]
+        wz_ref[...] = placed(jnp.where(gap < 0, gap + N, gap), spline_weights(frac[2:3, :]))
 
     def spread(stencil_ref, x, rows):
         along_x = wx_ref[pl.ds(x, 1), :]
@@ -216,20 +217,30 @@
         den_ref[x, 0:3 * N] += spread(sn_ref, x, 3)
         return carry
 
-    weigh(par_ref, pi, 0.0)
+    settle(("load", 0), ("load", 1))
+    weigh(frac_ref, base_ref, live_ref, pi, 0)
+    settle(("load", 2), ("load", 3))
     vals_ref[...] = both_ref[...].T
     lax.fori_loop(0, 7, own_plane, 0)
-    settle(("load", 4), ("shift", 0), ("shift", 1))
-    weigh(near_par_ref, lax.rem(pi + G - 1, G), 4.0)
+    settle(("load", 4), *[("shift", i) for i in range(5)])
+    weigh(near_frac_ref, near_base_ref, near_live_ref, lax.rem(pi + G - 1, G), 4)
     vals_ref[...] = near_ref[...].T
     lax.fori_loop(0, 7, near_plane, 0)
+    def in_halves(out):
+        return [out[h * R // 2:(h + 1) * R // 2].astype(BF16).reshape(G, 8, L) for h in range(2)]
+
+    def of_halves(ref, x):
+        return jnp.concatenate([ref[h, :, x].reshape(R // 2, L) for h in range(2)], axis=0)
+
     for x in range(0, 7, 2):
         pieces = [den_ref[i] for i in range(x, min(x + 2, 7))]
         for i, out in enumerate(stage(za_ref[...], pieces)):
-            s0_ref[:, x + i] = out.astype(BF16).reshape(G, 16, L)
-    begin(0, s0_ref, r0_ref, "slab")
-
-    settle(*[("load", i) for i in range(5, 11)])
+            for h, part in enumerate(in_halves(out)):
+                s0_ref[h, :, x + i] = part
+    for h in range(2):
+        begin(h, s0_ref.at[h], r0_ref.at[h], "slab")
+
+    settle(*[("load", i) for i in range(5, 12)])
     at = lax.broadcasted_iota(jnp.int32, (NB, 16 * N), 1)
     along = at // 4 % N
     kappa_sq = (
@@ -245,27 +256,35 @@
         precision=lax.Precision.HIGHEST, preferred_element_type=F32,
     ).reshape(4, R, L)
 
-    finish(0)
-    wide_ref[...] = r0_ref[...].reshape(7 * 16 * G, L).astype(F32)
-    for b in range(0, 16, 2):
-        outs = stage(xa_ref[...], [wide_ref[pl.ds(b + i, 7 * G, stride=16), :] for i in range(2)])
+    for h in range(2):
+        finish(h)
+        lo, hi = h * 56 * G, h * 8 * N
+        wide_ref[lo:lo + 56 * G, :] = r0_ref[h].reshape(56 * G, L).astype(F32)
+        for b in range(0, 8, 2):
+            outs = stage(xa_ref[...], [wide_ref[pl.ds(lo + b + i, 7 * G, stride=8), :] for i in range(2)])
+            for i in range(2):
+                line_ref[pl.ds(hi + b + i, N, stride=8), :] = outs[i]
+        s1_ref[h] = line_ref[hi:hi + 8 * N, :].astype(BF16).reshape(G, 4, 8, L)
+        begin(2 + h, s1_ref.at[h], r1_ref.at[h], "pencil")
+    finish(2)
+    finish(3)
+
+    for x in range(0, 4, 2):
+        outs = stage(ya_ref[...], [of_halves(r1_ref, x + i) for i in range(2)])
         for i in range(2):
-            line_ref[pl.ds(b + i, N, stride=16), :] = outs[i]
-    s1_ref[...] = line_ref[...].astype(BF16).reshape(G, 4, 16, L)
-    begin(1, s1_ref, r1_ref, "pencil")
-    finish(1)
+            spec_ref[x + i] = outs[i]
+        outs = stage(yb_ref[...], [outs[i] * prof_ref[x + i] for i in range(2)])
+        for i in range(2):
+            for h, part in enumerate(in_halves(outs[i])):
+                s2_ref[h, :, x + i] = part
+    for h in range(2):
+        begin(4 + h, s2_ref.at[h], r2_ref.at[h], "pencil")
 
     flip = jnp.where(si == 0, 1, 0)
     for x in range(0, 4, 2):
-        outs = stage(ya_ref[flip], [r1_ref[:, x + i].reshape(R, L) for i in range(2)])
+        outs = stage(ym_ref[flip], [of_halves(r1_ref, x + i) for i in range(2)])
         for i in range(2):
-            spec_ref[x + i] = outs[i][:R]
-            mirror_ref[x + i] = outs[i][R:]
-        outs = stage(yb_ref[...], [spec_ref[x + i] * prof_ref[x + i] for i in range(2)])
-        for i in range(2):
-            s2_ref[:, x + i] = outs[i].astype(BF16).reshape(G, 16, L)
-    begin(2, s2_ref, r2_ref, "pencil")
-
+            mirror_ref[x + i] = outs[i]
     for x in range(4):
         opposite = jnp.where(pi == 0, (4 - x) % 4, (x + 2) % 4)
         corr_ref[pl.ds(x * R, R), :] = spec_ref[x] * pltpu.roll(mirror_ref[opposite], C, 1)
@@ -277,27 +296,30 @@
     g1s_ref[...] = jnp.zeros_like(g1s_ref)
     for g in range(G):
         g1s_ref[g, 0:rows, :] = partial[g * rows:(g + 1) * rows]
-    exchange(4, lambda peer: g1s_ref.at[peer], g1r_ref, "pencil")
+    exchange(8, lambda peer: g1s_ref.at[peer], g1r_ref, "pencil")
     g1r_ref[pl.ds(pi, 1)] = g1s_ref[pl.ds(pi, 1)]
 
-    finish(2)
-    line_ref[...] = r2_ref[...].reshape(16 * N, L).astype(F32)
-    for b in range(0, 16, 2):
-        outs = stage(xb_ref[...], [line_ref[pl.ds(b + i, N, stride=16), :] for i in range(2)])
-        for i in range(2):
-            wide_ref[pl.ds(b + i, 7 * G, stride=16), :] = outs[i]
-    s3_ref[...] = wide_ref[...].astype(BF16).reshape(G, 7, 16, L)
-    begin(3, s3_ref, r3_ref, "slab")
-
-    settle(("exchange", 4))
+    for h in range(2):
+        finish(4 + h)
+        lo, hi = h * 56 * G, h * 8 * N
+        line_ref[hi:hi + 8 * N, :] = r2_ref[h].reshape(8 * N, L).astype(F32)
+        for b in range(0, 8, 2):
+            outs = stage(xb_ref[...], [line_ref[pl.ds(hi + b + i, N, stride=8), :] for i in range(2)])
+            for i in range(2):
+                wide_ref[pl.ds(lo + b + i, 7 * G, stride=8), :] = outs[i]
+        s3_ref[h] = wide_ref[lo:lo + 56 * G, :].astype(BF16).reshape(G, 7, 8, L)
+        begin(6 + h, s3_ref.at[h], r3_ref.at[h], "slab")
+
+    settle(("exchange", 8))
     total = jnp.sum(g1r_ref[...], axis=0)
     g2s_ref[...] = total
-    exchange(5, lambda peer: g2s_ref, g2r_ref, "slab")
+    exchange(9, lambda peer: g2s_ref, g2r_ref, "slab")
     g2r_ref[pl.ds(si, 1)] = total[None]
 
-    finish(3)
+    finish(6)
+    finish(7)
     for x in range(0, 7, 2):
-        pieces = [r3_ref[:, i].reshape(R, L) for i in range(x, min(x + 2, 7))]
+        pieces = [of_halves(r3_ref, i) for i in range(x, min(x + 2, 7))]
         for i, out in enumerate(stage(zb_ref[...], pieces)):
             field_ref[x + i] = out.astype(BF16)
 
@@ -309,24 +331,33 @@
         )
 
     part_ref[...] = gathered(sn_ref, 3).astype(BF16)
-    shift(2, part_ref, back_ref, -1)
-
-    settle(("exchange", 5))
+    shift(5, part_ref, back_ref, -1)
+
+    settle(("exchange", 9))
     total = jnp.sum(g2r_ref[...], axis=0)
     g3s_ref[...] = total
-    exchange(6, lambda peer: g3s_ref, g3r_ref, "pencil")
+    exchange(10, lambda peer: g3s_ref, g3r_ref, "pencil")
     g3r_ref[pl.ds(pi, 1)] = total[None]
 
     acc_ref[...] = gathered(st_ref, 4)
-    settle(("shift", 2))
+    settle(("shift", 5))
     pot_ref[...] = (acc_ref[0:C] + back_ref[0:C].astype(F32)).astype(BF16)
     cg_ref[...] = (acc_ref[C:L] + back_ref[C:L].astype(F32)).astype(BF16)
 
-    settle(("exchange", 6))
+    settle(("exchange", 10))
     for g in range(G):
         grad_ref[g * rows:(g + 1) * rows, :] = g3r_ref[g, 0:rows, 0:C]
     for wait in owed.values():
         wait()
+
+
+def deliver(pot_ref, cg_ref, grad_ref, pot_out, cg_out, grad_out, sems):
+    pairs = [(pot_ref, pot_out), (cg_ref, cg_out), (grad_ref, grad_out)]
+    copies = [pltpu.make_async_copy(src, dst, sems.at[i]) for i, (src, dst) in enumerate(pairs)]
+    for copy in copies:
+        copy.start()
+    for copy in copies:
+        copy.wait()
 
 
 def per_device(charges, cotangent, base_cell, frac, counts, filter_weights):
@@ -337,8 +368,8 @@
     vmem = pl.BlockSpec(memory_space=pltpu.VMEM)
     smem = pl.BlockSpec(memory_space=pltpu.SMEM)
     hbm = pl.BlockSpec(memory_space=pltpu.HBM)
-    wide = pltpu.VMEM((G, 7, 16, L), BF16)
-    slim = pltpu.VMEM((G, 4, 16, L), BF16)
+    wide = pltpu.VMEM((2, G, 7, 8, L), BF16)
+    slim = pltpu.VMEM((2, G, 4, 8, L), BF16)
     tiles = pltpu.VMEM((G, 8, L), F32)
     tile = pltpu.VMEM((8, L), F32)
     scratch = [
@@ -347,9 +378,11 @@
         pltpu.VMEM((L, slots), BF16),
         pltpu.VMEM((NB, C), F32),
         *[pltpu.VMEM(t.shape, BF16) for t in dft],
-        pltpu.SemaphoreType.DMA((11,)),
+        pltpu.SemaphoreType.DMA((12,)),
         pltpu.VMEM((8, slots), F32),
         pltpu.VMEM((8, slots), F32),
+        pltpu.VMEM((3, slots), F32),
+        pltpu.VMEM((3, slots), jnp.int32),
         pltpu.VMEM((L, slots), BF16),
         pltpu.VMEM((8, slots), F32),
         pltpu.VMEM((8, slots), F32),
@@ -371,26 +404,35 @@
         pltpu.VMEM((L, slots), BF16),
         pltpu.VMEM((L, slots), BF16),
         tiles, tiles, tile, tiles, tile, tiles,
-        pltpu.SemaphoreType.DMA((3,)),
-        pltpu.SemaphoreType.DMA((3,)),
-        pltpu.SemaphoreType.DMA((7,)),
-        pltpu.SemaphoreType.DMA((7,)),
-        pltpu.SemaphoreType.DMA((4,)),
+        pltpu.SemaphoreType.DMA((6,)),
+        pltpu.SemaphoreType.DMA((6,)),
+        pltpu.SemaphoreType.DMA((11,)),
+        pltpu.SemaphoreType.DMA((11,)),
+        pltpu.SemaphoreType.DMA((8,)),
     ]
-    return pl.pallas_call(
+    shapes = (
+        jax.ShapeDtypeStruct((C, slots), BF16),
+        jax.ShapeDtypeStruct((C, slots), BF16),
+        jax.ShapeDtypeStruct((NB, C), F32),
+    )
+    results = pl.pallas_call(
         functools.partial(kernel, G),
-        out_shape=(
-            jax.ShapeDtypeStruct((C, slots), BF16),
-            jax.ShapeDtypeStruct((C, slots), BF16),
-            jax.ShapeDtypeStruct((NB, C), F32),
-        ),
-        in_specs=[smem] + [hbm] * 11,
+        out_shape=shapes,
+        in_specs=[smem] + [hbm] * 12,
         out_specs=(vmem, vmem, vmem),
         scratch_shapes=scratch,
         compiler_params=pltpu.CompilerParams(
             collective_id=0, has_side_effects=True, vmem_limit_bytes=67043328
         ),
     )(counts, charges, cotangent, base_cell, frac, filter_weights, *dft)
+    return pl.pallas_call(
+        deliver,
+        out_shape=shapes,
+        in_specs=[hbm] * 3,
+        out_specs=(vmem, vmem, vmem),
+        scratch_shapes=[pltpu.SemaphoreType.DMA((3,))],
+        compiler_params=pltpu.CompilerParams(vmem_limit_bytes=67043328),
+    )(*results)
 
 
 def solution(mesh):

time: 57.7 us -> 54 us (0.936)
  local copies, waits for them, and re-layouts: 2.83 us -> 0 us
  Pallas kernels: 53.3 us -> 52.6 us
    unnamed x7 -> x0, local copies, waits for them, and re-layouts: 2.83 us -> none
    pallas_call x1 -> x2, Pallas kernels: 53.3 us -> 52.6 us  [the longest x1 51 us: per_device(): pl.pallas_call(functools.partial(kernel, G), out_shape=shapes, in_specs=[...]
where the time goes in v5:
time: 54 us; the launch traced here: 53.8 us
  Pallas kernels  52.6 us (97%)
  between operations  1.29 us (2%)
    pallas_call x1, Pallas kernels, per_device(): pl.pallas_call(functools.partial(kernel, G), out_shape=shapes, in_specs=[...  51 us
    pallas_call x1, Pallas kernels, per_device(): pl.pallas_call(deliver, out_shape=shapes, in_specs=[hbm] * 3, out_specs=(...  1.55 us

profile of v5, /device:TPU:1, one launch (start us, length us, event | category | flops | bytes accessed | tf_op | source)
XLA Modules:
  0.0 53.8 jit_solution(11557471076142190982)
XLA Ops:
  1.3 51.0 %shard_map.148 = (bf16[64,512]{1,0:T(8,128)(2,1)}, bf16[64,512]{1,0:T(8,128)(2,1)}, f32[32,64]{1,0:T(8,128)}) custom-call(s32[1]{0:T(128)S(6)} %copy.16.count_ref, bf16[64,512]{1,0:T(8,128)(2,1)} %charges_hbm.1, bf16[64,512]{1,0:T(8,128)(2,1)} %cot_hbm.1, s32[3,512]{1,0:T(4,128)} %base_hbm.1, f32[3,512]{1,0:T(4,128)} %frac_hbm.1, f32[32,64]{1,0:T(8,128)} %weights_hbm.1, ...), custom_call_target="tpu_custom_call" | custom-call | tf_op jit(solution)/shard_map/pallas_call | solution.py:418
  52.3 1.6 %shard_map.149 = (bf16[64,512]{1,0:T(8,128)(2,1)}, bf16[64,512]{1,0:T(8,128)(2,1)}, f32[32,64]{1,0:T(8,128)}) custom-call(bf16[64,512]{1,0:T(8,128)(2,1)} %get-tuple-element.6.pot_ref, bf16[64,512]{1,0:T(8,128)(2,1)} %get-tuple-element.7.cg_ref, f32[32,64]{1,0:T(8,128)} %get-tuple-element.8.grad_ref), custom_call_target="tpu_custom_call" | custom-call | tf_op jit(solution)/shard_map/pallas_call | solution.py:428

commit v6 on v5

--- a/solution.py
+++ b/solution.py
@@ -37,7 +37,7 @@
         return (cosines.T / count, -sines.T / count) if inverse else (cosines, sines)
 
     def joined(pair, pattern=None, inner=eye):
-        size = 4 * count
+        size = inner.shape[0] * count
         if pattern is not None:
             split = [t.reshape(groups, 4, groups, 4) for t in pair]
             pair = [np.einsum(pattern, t, inner).reshape(size, size) for t in split]
@@ -52,13 +52,13 @@
     halves = np.arange(4 * count).reshape(groups, 2, 2, 4).transpose(1, 0, 2, 3).reshape(-1)
     paired = np.concatenate([halves, halves + 4 * count])
     made = [
-        joined(ahead, "glhm,yv->gylvhm")[halves],
+        joined(ahead, "glhm,yv->gylvhm", np.eye(2)),
         joined(parts(waves, wide, False)),
         y_ahead[:, paired],
         np.stack([joined(mirror, "glhm,ab->glahmb", t)[:, paired] for t in across]),
         joined(back, "glhm,ab->glahmb")[halves],
         joined(parts(waves, wide, True)),
-        joined(back, "glhm,yv->yglhvm")[:, paired],
+        joined(back, "glhm,yv->yglhvm", np.eye(2)),
     ]
     return [jnp.asarray(t, BF16) for t in made]
 
@@ -104,7 +104,7 @@
     base_ref, frac_ref, both_ref, weights_ref, za_ref, xa_ref, ya_ref, ym_ref, yb_ref, xb_ref, zb_ref, load_sem,
     live_ref, near_live_ref, near_frac_ref, near_base_ref, near_ref, wx_ref, wy_ref, wz_ref, st_ref, sn_ref, vals_ref, den_ref,
     s0_ref, r0_ref, s1_ref, r1_ref, s2_ref, r2_ref, s3_ref, r3_ref,
-    wide_ref, line_ref, spec_ref, mirror_ref, prof_ref, shell_ref, corr_ref, field_ref, acc_ref, part_ref, back_ref,
+    wide_ref, line_ref, spec_ref, mirror_ref, prof_ref, shell_ref, corr_ref, field_ref, acc_ref, near_acc_ref, part_ref, back_ref,
     g1s_ref, g1r_ref, g2s_ref, g2r_ref, g3s_ref, g3r_ref,
     hs, hr, es, er, local_sem,
 ):
@@ -202,20 +202,23 @@
         gap = lax.broadcasted_iota(jnp.int32, (N, slots), 0) - base[2:3, :]
         wz_ref[...] = placed(jnp.where(gap < 0, gap + N, gap), spline_weights(frac[2:3, :]))
 
-    def spread(stencil_ref, x, rows):
+    def spread(stencil_ref, x, first, last):
         along_x = wx_ref[pl.ds(x, 1), :]
-        for y in range(rows):
+        for y in range(first, last):
             stencil_ref[x, y] = (wz_ref[...] * (along_x * wy_ref[y:y + 1, :])).astype(BF16)
-        left = stencil_ref[x].reshape(rows * N, slots)
+        left = stencil_ref[x, first:last].reshape((last - first) * N, slots)
         return jnp.dot(left, vals_ref[...], preferred_element_type=F32)
 
     def own_plane(x, carry):
-        den_ref[x] = spread(st_ref, x, 4)
+        den_ref[x] = spread(st_ref, x, 0, 4)
         return carry
 
-    def near_plane(x, carry):
-        den_ref[x, 0:3 * N] += spread(sn_ref, x, 3)
-        return carry
+    def near_plane(first, last):
+        def add(x, carry):
+            den_ref[x, first * N:last * N] += spread(sn_ref, x, first, last)
+            return carry
+
+        return add
 
     settle(("load", 0), ("load", 1))
     weigh(frac_ref, base_ref, live_ref, pi, 0)
@@ -225,19 +228,18 @@
     settle(("load", 4), *[("shift", i) for i in range(5)])
     weigh(near_frac_ref, near_base_ref, near_live_ref, lax.rem(pi + G - 1, G), 4)
     vals_ref[...] = near_ref[...].T
-    lax.fori_loop(0, 7, near_plane, 0)
     def in_halves(out):
         return [out[h * R // 2:(h + 1) * R // 2].astype(BF16).reshape(G, 8, L) for h in range(2)]
 
     def of_halves(ref, x):
         return jnp.concatenate([ref[h, :, x].reshape(R // 2, L) for h in range(2)], axis=0)
 
-    for x in range(0, 7, 2):
-        pieces = [den_ref[i] for i in range(x, min(x + 2, 7))]
-        for i, out in enumerate(stage(za_ref[...], pieces)):
-            for h, part in enumerate(in_halves(out)):
-                s0_ref[h, :, x + i] = part
     for h in range(2):
+        lax.fori_loop(0, 7, near_plane(2 * h, min(2 * h + 2, 3)), 0)
+        for x in range(0, 7, 2):
+            pieces = [den_ref[i, h * R // 2:(h + 1) * R // 2] for i in range(x, min(x + 2, 7))]
+            for i, out in enumerate(stage(za_ref[...], pieces)):
+                s0_ref[h, :, x + i] = out.astype(BF16).reshape(G, 8, L)
         begin(h, s0_ref.at[h], r0_ref.at[h], "slab")
 
     settle(*[("load", i) for i in range(5, 12)])
@@ -293,9 +295,8 @@
     )
     partial = (partial + pltpu.roll(partial, C, 1)) * (0.5 / (N * N * N))
     rows = NB // G
-    g1s_ref[...] = jnp.zeros_like(g1s_ref)
     for g in range(G):
-        g1s_ref[g, 0:rows, :] = partial[g * rows:(g + 1) * rows]
+        g1s_ref[g] = partial[g * rows:(g + 1) * rows]
     exchange(8, lambda peer: g1s_ref.at[peer], g1r_ref, "pencil")
     g1r_ref[pl.ds(pi, 1)] = g1s_ref[pl.ds(pi, 1)]
 
@@ -316,21 +317,26 @@
     exchange(9, lambda peer: g2s_ref, g2r_ref, "slab")
     g2r_ref[pl.ds(si, 1)] = total[None]
 
-    finish(6)
-    finish(7)
-    for x in range(0, 7, 2):
-        pieces = [of_halves(r3_ref, i) for i in range(x, min(x + 2, 7))]
-        for i, out in enumerate(stage(zb_ref[...], pieces)):
-            field_ref[x + i] = out.astype(BF16)
-
-    def gathered(stencil_ref, rows):
-        depth = 7 * rows * N
+    def gathered(stencil_ref, first, last):
+        depth = 7 * (last - first) * N
         return lax.dot_general(
-            field_ref[:, 0:rows * N].reshape(depth, L), stencil_ref[...].reshape(depth, slots),
+            field_ref[:, first * N:last * N].reshape(depth, L), stencil_ref[:, first:last].reshape(depth, slots),
             (((0,), (0,)), ((), ())), preferred_element_type=F32,
         )
 
-    part_ref[...] = gathered(sn_ref, 3).astype(BF16)
+    def field_half(h):
+        for x in range(0, 7, 2):
+            pieces = [r3_ref[h, :, i].reshape(R // 2, L) for i in range(x, min(x + 2, 7))]
+            for i, out in enumerate(stage(zb_ref[...], pieces)):
+                field_ref[x + i, h * R // 2:(h + 1) * R // 2] = out.astype(BF16)
+
+    finish(6)
+    field_half(0)
+    near_acc_ref[...] = gathered(sn_ref, 0, 2)
+    acc_ref[...] = gathered(st_ref, 0, 2)
+    finish(7)
+    field_half(1)
+    part_ref[...] = (near_acc_ref[...] + gathered(sn_ref, 2, 3)).astype(BF16)
     shift(5, part_ref, back_ref, -1)
 
     settle(("exchange", 9))
@@ -339,14 +345,14 @@
     exchange(10, lambda peer: g3s_ref, g3r_ref, "pencil")
     g3r_ref[pl.ds(pi, 1)] = total[None]
 
-    acc_ref[...] = gathered(st_ref, 4)
+    acc_ref[...] += gathered(st_ref, 2, 4)
     settle(("shift", 5))
     pot_ref[...] = (acc_ref[0:C] + back_ref[0:C].astype(F32)).astype(BF16)
     cg_ref[...] = (acc_ref[C:L] + back_ref[C:L].astype(F32)).astype(BF16)
 
     settle(("exchange", 10))
     for g in range(G):
-        grad_ref[g * rows:(g + 1) * rows, :] = g3r_ref[g, 0:rows, 0:C]
+        grad_ref[g * rows:(g + 1) * rows, :] = g3r_ref[g, :, 0:C]
     for wait in owed.values():
         wait()
 
@@ -370,8 +376,8 @@
     hbm = pl.BlockSpec(memory_space=pltpu.HBM)
     wide = pltpu.VMEM((2, G, 7, 8, L), BF16)
     slim = pltpu.VMEM((2, G, 4, 8, L), BF16)
-    tiles = pltpu.VMEM((G, 8, L), F32)
-    tile = pltpu.VMEM((8, L), F32)
+    tiles = pltpu.VMEM((G, NB // G, L), F32)
+    tile = pltpu.VMEM((NB // G, L), F32)
     scratch = [
         pltpu.VMEM((3, slots), jnp.int32),
         pltpu.VMEM((3, slots), F32),
@@ -400,6 +406,7 @@
         pltpu.VMEM((NB, 16 * N), F32),
         pltpu.VMEM((16 * N, L), F32),
         pltpu.VMEM((7, 4 * N, L), BF16),
+        pltpu.VMEM((L, slots), F32),
         pltpu.VMEM((L, slots), F32),
         pltpu.VMEM((L, slots), BF16),
         pltpu.VMEM((L, slots), BF16),

time: 54 us -> 53.1 us (0.983)
  Pallas kernels: 52.6 us -> 51.7 us
    pallas_call x1, Pallas kernels: 51 us -> 50.1 us  [per_device(): pl.pallas_call(functools.partial(kernel, G), out_shape=shapes, in_specs=[...]
where the time goes in v6:
time: 53.1 us; the launch traced here: 52.9 us
  Pallas kernels  51.7 us (97%)
  between operations  1.29 us (2%)
    pallas_call x1, Pallas kernels, per_device(): pl.pallas_call(functools.partial(kernel, G), out_shape=shapes, in_specs=[...  50.1 us
    pallas_call x1, Pallas kernels, per_device(): pl.pallas_call(deliver, out_shape=shapes, in_specs=[hbm] * 3, out_specs=(...  1.55 us

profile of v6, /device:TPU:1, one launch (start us, length us, event | category | flops | bytes accessed | tf_op | source)
XLA Modules:
  0.0 52.9 jit_solution(1237428404129409671)
XLA Ops:
  1.3 50.1 %shard_map.148 = (bf16[64,512]{1,0:T(8,128)(2,1)}, bf16[64,512]{1,0:T(8,128)(2,1)}, f32[32,64]{1,0:T(8,128)}) custom-call(s32[1]{0:T(128)S(6)} %copy.16.count_ref, bf16[64,512]{1,0:T(8,128)(2,1)} %charges_hbm.1, bf16[64,512]{1,0:T(8,128)(2,1)} %cot_hbm.1, s32[3,512]{1,0:T(4,128)} %base_hbm.1, f32[3,512]{1,0:T(4,128)} %frac_hbm.1, f32[32,64]{1,0:T(8,128)} %weights_hbm.1, ...), custom_call_target="tpu_custom_call" | custom-call | tf_op jit(solution)/shard_map/pallas_call | solution.py:425
  51.4 1.6 %shard_map.149 = (bf16[64,512]{1,0:T(8,128)(2,1)}, bf16[64,512]{1,0:T(8,128)(2,1)}, f32[32,64]{1,0:T(8,128)}) custom-call(bf16[64,512]{1,0:T(8,128)(2,1)} %get-tuple-element.6.pot_ref, bf16[64,512]{1,0:T(8,128)(2,1)} %get-tuple-element.7.cg_ref, f32[32,64]{1,0:T(8,128)} %get-tuple-element.8.grad_ref), custom_call_target="tpu_custom_call" | custom-call | tf_op jit(solution)/shard_map/pallas_call | solution.py:435

commit v7 on v6

--- a/solution.py
+++ b/solution.py
@@ -189,11 +189,11 @@
     live = lax.broadcasted_iota(jnp.int32, (8, slots), 1) < count_ref[0]
     live_ref[...] = live.astype(F32)
     pl.semaphore_wait(barrier, 2 * (G - 1))
-    shift(0, charges_hbm, near_ref.at[0:C], 1)
-    shift(1, cot_hbm, near_ref.at[C:L], 1)
     shift(2, frac_hbm, near_frac_ref, 1)
     shift(3, base_hbm, near_base_ref, 1)
     shift(4, live_ref, near_live_ref, 1)
+    shift(0, charges_hbm, near_ref.at[0:C], 1)
+    shift(1, cot_hbm, near_ref.at[C:L], 1)
 
     def weigh(frac, base, alive, block, first_row):
         row = lax.broadcasted_iota(jnp.int32, (8, slots), 0)
@@ -202,15 +202,22 @@
         gap = lax.broadcasted_iota(jnp.int32, (N, slots), 0) - base[2:3, :]
         wz_ref[...] = placed(jnp.where(gap < 0, gap + N, gap), spline_weights(frac[2:3, :]))
 
+    def stencil_plane(stencil_ref, x, rows):
+        along_x = wx_ref[pl.ds(x, 1), :]
+        for y in range(rows):
+            stencil_ref[x, y] = (wz_ref[...] * (along_x * wy_ref[y:y + 1, :])).astype(BF16)
+
     def spread(stencil_ref, x, first, last):
-        along_x = wx_ref[pl.ds(x, 1), :]
-        for y in range(first, last):
-            stencil_ref[x, y] = (wz_ref[...] * (along_x * wy_ref[y:y + 1, :])).astype(BF16)
         left = stencil_ref[x, first:last].reshape((last - first) * N, slots)
         return jnp.dot(left, vals_ref[...], preferred_element_type=F32)
 
     def own_plane(x, carry):
+        stencil_plane(st_ref, x, 4)
         den_ref[x] = spread(st_ref, x, 0, 4)
+        return carry
+
+    def near_stencil(x, carry):
+        stencil_plane(sn_ref, x, 3)
         return carry
 
     def near_plane(first, last):
@@ -225,8 +232,10 @@
     settle(("load", 2), ("load", 3))
     vals_ref[...] = both_ref[...].T
     lax.fori_loop(0, 7, own_plane, 0)
-    settle(("load", 4), *[("shift", i) for i in range(5)])
+    settle(*[("shift", i) for i in range(2, 5)])
     weigh(near_frac_ref, near_base_ref, near_live_ref, lax.rem(pi + G - 1, G), 4)
+    lax.fori_loop(0, 7, near_stencil, 0)
+    settle(("load", 4), ("shift", 0), ("shift", 1))
     vals_ref[...] = near_ref[...].T
     def in_halves(out):
         return [out[h * R // 2:(h + 1) * R // 2].astype(BF16).reshape(G, 8, L) for h in range(2)]
@@ -235,7 +244,7 @@
         return jnp.concatenate([ref[h, :, x].reshape(R // 2, L) for h in range(2)], axis=0)
 
     for h in range(2):
-        lax.fori_loop(0, 7, near_plane(2 * h, min(2 * h + 2, 3)), 0)
+        lax.fori_loop(0, 7, near_plane(2 * h, min(2 * h + 2, 3)), 0, unroll=True)
         for x in range(0, 7, 2):
             pieces = [den_ref[i, h * R // 2:(h + 1) * R // 2] for i in range(x, min(x + 2, 7))]
             for i, out in enumerate(stage(za_ref[...], pieces)):

time: 53.1 us -> 52.1 us (0.981)
  Pallas kernels: 51.7 us -> 50.7 us
    pallas_call x1, Pallas kernels: 50.1 us -> 49.1 us  [per_device(): pl.pallas_call(functools.partial(kernel, G), out_shape=shapes, in_specs=[...]
where the time goes in v7:
time: 52.1 us; the launch traced here: 52 us
  Pallas kernels  50.7 us (97%)
  between operations  1.29 us (2%)
    pallas_call x1, Pallas kernels, per_device(): pl.pallas_call(functools.partial(kernel, G), out_shape=shapes, in_specs=[...  49.1 us
    pallas_call x1, Pallas kernels, per_device(): pl.pallas_call(deliver, out_shape=shapes, in_specs=[hbm] * 3, out_specs=(...  1.55 us

profile of v7, /device:TPU:1, one launch (start us, length us, event | category | flops | bytes accessed | tf_op | source)
XLA Modules:
  0.0 52.0 jit_solution(15977093987099232086)
XLA Ops:
  1.3 49.1 %shard_map.148 = (bf16[64,512]{1,0:T(8,128)(2,1)}, bf16[64,512]{1,0:T(8,128)(2,1)}, f32[32,64]{1,0:T(8,128)}) custom-call(s32[1]{0:T(128)S(6)} %copy.16.count_ref, bf16[64,512]{1,0:T(8,128)(2,1)} %charges_hbm.1, bf16[64,512]{1,0:T(8,128)(2,1)} %cot_hbm.1, s32[3,512]{1,0:T(4,128)} %base_hbm.1, f32[3,512]{1,0:T(4,128)} %frac_hbm.1, f32[32,64]{1,0:T(8,128)} %weights_hbm.1, ...), custom_call_target="tpu_custom_call" | custom-call | tf_op jit(solution)/shard_map/pallas_call | solution.py:434
  50.4 1.6 %shard_map.149 = (bf16[64,512]{1,0:T(8,128)(2,1)}, bf16[64,512]{1,0:T(8,128)(2,1)}, f32[32,64]{1,0:T(8,128)}) custom-call(bf16[64,512]{1,0:T(8,128)(2,1)} %get-tuple-element.6.pot_ref, bf16[64,512]{1,0:T(8,128)(2,1)} %get-tuple-element.7.cg_ref, f32[32,64]{1,0:T(8,128)} %get-tuple-element.8.grad_ref), custom_call_target="tpu_custom_call" | custom-call | tf_op jit(solution)/shard_map/pallas_call | solution.py:444
